TPU v7x, 256 devices: a whole 4x4x8 slice. The times are simulated.
256 devices in a mesh: band: 4 (over y_lo, core), slab: 64 (over z, y_hi, x).
Axes of the slice: x: 4, y: 4 (y_hi: 2, y_lo: 2; y = y_hi * 2 + y_lo), z: 8, core: 2. Of those that a mesh axis runs over, the one named last changes fastest.
Arguments:
- bands: float32 [8, 192, 192, 192], P('band', 'slab'), may hold values from -8 to 8
- occupied: float32 [16, 192, 192, 192], P('band', 'slab'), may hold values from -8 to 8
- occ_index: int32 [2], replicated, may hold values from 0 to 15
- band_pick: int32 [8], P('band'), may hold values from 0 to 1
Outputs:
- exchange_out: float32 [8, 192, 192, 192], P('band', 'slab')
All inputs are finite; a program needn't handle non-finite values.
Results may differ from a plain program's by a relative error of at most 0.0001.
Values sent between devices are 32-bit elements; how exact they have to be, the bound alone decides.
A program may use at most 64 MiB of HBM per device.

v0:
```python
import math

import jax
import jax.numpy as jnp
from jax import lax
from jax.sharding import PartitionSpec as P

grid_step = 0.25
omega = 0.106


def broadcast(x, axis, root):
    mine = lax.axis_index(axis) == root
    return lax.psum(jnp.where(mine, x, jnp.zeros_like(x)), axis)


def wave_squared(length):
    modes = jnp.arange(length, dtype=jnp.int32)
    signed = jnp.where(modes <= length // 2, modes, modes - length)
    wave = 2.0 * math.pi / (length * grid_step) * signed.astype(jnp.float32)
    return wave * wave


def screened(squares):
    nonzero = jnp.where(squares > 0, squares, jnp.ones_like(squares))
    value = 4.0 * math.pi * (1.0 - jnp.exp(-squares / (4.0 * omega * omega))) / nonzero
    return jnp.where(squares > 0, value, jnp.full_like(squares, math.pi / (omega * omega)))


def cas_matrix(length):
    indices = jnp.arange(length, dtype=jnp.int32)
    product = indices[:, None] * indices[None, :] % length
    phases = 2.0 * math.pi / length * product.astype(jnp.float32)
    return jnp.cos(phases) + jnp.sin(phases)


def along_z(values, matrix):
    return jnp.einsum("pxyz,zk->pxyk", values, matrix, precision=lax.Precision.HIGHEST)


def along_y(values, matrix):
    return jnp.einsum("pxyz,yk->pxkz", values, matrix, precision=lax.Precision.HIGHEST)


def along_x(values, matrix):
    return jnp.einsum("pxyz,xk->pkyz", values, matrix, precision=lax.Precision.HIGHEST)


def shards(bands, occupied, occ_index, band_pick):
    points = bands.shape[2]
    planes = bands.shape[1]
    window = occ_index.shape[0]
    per_group = occupied.shape[0]
    matrix = cas_matrix(points)
    squares = wave_squared(points)
    offset = lax.axis_index("slab") * planes
    row_squares = lax.dynamic_slice_in_dim(squares, offset, planes)
    kernel = screened(squares[:, None, None] + row_squares[None, :, None] + squares[None, None, :])
    kernel = kernel / float(points * points * points)
    targets = jnp.take(bands, band_pick, axis=0)

    def fetch_orbital(turn):
        which = occ_index[turn]
        owner_group = which // per_group
        own_orbital = lax.dynamic_index_in_dim(occupied, which % per_group, 0, keepdims=False)
        return broadcast(own_orbital, "band", owner_group)

    def to_spectrum(density):
        return along_y(along_z(density, matrix), matrix)

    def from_spectrum(spectrum):
        return along_z(along_y(spectrum, matrix), matrix)

    def convolve(pencil):
        return along_x(kernel[None] * along_x(pencil, matrix), matrix)

    def back_each(pencil):
        return lax.all_to_all(convolve(pencil), "slab", split_axis=1, concat_axis=2, tiled=True)

    def update(turn, total):
        orbital = fetch_orbital(turn)
        density = targets * orbital[None]
        filtered = back_each(
            lax.all_to_all(to_spectrum(density), "slab", split_axis=2, concat_axis=1, tiled=True)
        )
        return total - from_spectrum(filtered) * orbital[None]

    result = lax.fori_loop(0, window, update, jnp.zeros(targets.shape, jnp.float32))
    return result


def solution(mesh):
    placed = (P("band", "slab", None, None), P("band", "slab", None, None), P(), P("band"))
    return jax.shard_map(
        shards, mesh=mesh, in_specs=placed, out_specs=P("band", "slab", None, None), check_vma=False
    )
```

profile of v0, /device:TPU:8, one launch (start us, length us, event | category | flops | bytes accessed | tf_op | source)
XLA Modules:
  0.0 319.7 jit_solution(7959825404634566891)
XLA Ops:
  9.1 303.7 %while.17 = (s32[]{:T(128)}, f32[2,3,192,192]{3,2,1,0:T(8,128)}, s32[2]{0:T(128)S(1)}, f32[4,3,192,192]{3,2,1,0:T(8,128)}, f32[2,3,192,192]{3,2,1,0:T(8,128)S(1)...) while((s32[]{:T(128)}, f32[2,3,192,192]{3,2,1,0:T(8,128)}, ...), condition=%wide.region_2.3_spmd.clone.clone, body=%wide.region_0.2_spmd.clone.clone.sunk | while | flops 3062292480 | bytes 46599840 | solution.py:88
  12.0 1.9 select_bitcast_fusion.2
  14.0 45.6 %all-reduce.2.cloned.1.call-done = f32[3,192,192]{2,1,0:T(8,128)} async-done(((f32[3,192,192]{2,1,0:T(8,128)}), f32[3,192,192]{2,1,0:T(8,128)}) %all-reduce.2.cloned.1.call-update) | async-done | bytes 442384 | tf_op jit(solution)/shard_map/while/body/eval_jaxpr/psum | solution.py:14
  59.6 3.1 fusion.81
  62.7 1.9 convolution_bitcast_fusion.7
  66.2 12.1 %all-to-all-start = ((f32[2,3,192,192]{3,0,1,2:T(2,128)}), f32[2,3,192,192]{3,0,1,2:T(2,128)S(1)}, u32[]{:S(2)}, u32[]{:S(2)}) async-start(f32[2,3,192,192]{3,0,1,2:T(2,128)} %copy.44), calls=%async_computation | async-start | bytes 2359296 | tf_op jit(solution)/shard_map/while/body/eval_jaxpr/all_to_all | solution.py:84
  78.6 31.9 %all-to-all-done = f32[2,3,192,192]{3,0,1,2:T(2,128)S(1)} async-done(((f32[2,3,192,192]{3,0,1,2:T(2,128)}), f32[2,3,192,192]{3,0,1,2:T(2,128)S(1)}, u32[]{:S(2)}, u32[]{:S(2)}) %all-to-all-start) | async-done | bytes 884768 | tf_op jit(solution)/shard_map/while/body/eval_jaxpr/all_to_all | solution.py:84
  110.9 3.0 fusion.83
  114.0 1.9 convolution_bitcast_fusion.8
  117.5 7.4 %all-to-all-start.1 = ((f32[2,192,3,192]{3,0,2,1:T(2,128)}), f32[2,192,3,192]{3,0,2,1:T(2,128)S(1)}, u32[]{:S(2)}, u32[]{:S(2)}) async-start(f32[2,192,3,192]{3,0,2,1:T(2,128)} %copy.46), calls=%async_computation.1 | async-start | bytes 2359296 | tf_op jit(solution)/shard_map/while/body/eval_jaxpr/all_to_all | solution.py:78
  124.9 31.2 %all-to-all-done.1 = f32[2,192,3,192]{3,0,2,1:T(2,128)S(1)} async-done(((f32[2,192,3,192]{3,0,2,1:T(2,128)}), f32[2,192,3,192]{3,0,2,1:T(2,128)S(1)}, u32[]{:S(2)}, u32[]{:S(2)}) %all-to-all-start.1) | async-done | bytes 884768 | tf_op jit(solution)/shard_map/while/body/eval_jaxpr/all_to_all | solution.py:78
  156.5 3.0 convolution_bitcast_fusion.9
  159.6 3.4 %fusion.84 = f32[2,3,192,192]{3,2,1,0:T(8,128)S(1)} fusion(f32[2,3,192,192]{2,3,1,0:T(8,128)S(1)} %convolution_bitcast_fusion.9, f32[2,3,192,192]{3,2,1,0:T(8,128)S(1)} %copy-done.4, f32[3,192,192]{2,1,0:T(8,128)S(1)} %copy-done.1, pred[]{:T(512)S(6)} %compare.14), kind=kOutput, calls=%fused_computation.4.clone.1 | convolution fusion | flops 510640128 | bytes 3096577 | tf_op jit(solution)/shard_map/while/body/eval_jaxpr/pxyz,zk->pxyk/dot_general | solution.py:38
  166.8 1.9 select_bitcast_fusion.2
  168.8 39.6 %all-reduce.2.cloned.1.call-done = f32[3,192,192]{2,1,0:T(8,128)} async-done(((f32[3,192,192]{2,1,0:T(8,128)}), f32[3,192,192]{2,1,0:T(8,128)}) %all-reduce.2.cloned.1.call-update) | async-done | bytes 442384 | tf_op jit(solution)/shard_map/while/body/eval_jaxpr/psum | solution.py:14
  208.5 3.1 fusion.81
  211.6 1.9 convolution_bitcast_fusion.7
  215.1 12.1 %all-to-all-start = ((f32[2,3,192,192]{3,0,1,2:T(2,128)}), f32[2,3,192,192]{3,0,1,2:T(2,128)S(1)}, u32[]{:S(2)}, u32[]{:S(2)}) async-start(f32[2,3,192,192]{3,0,1,2:T(2,128)} %copy.44), calls=%async_computation | async-start | bytes 2359296 | tf_op jit(solution)/shard_map/while/body/eval_jaxpr/all_to_all | solution.py:84
  227.5 31.9 %all-to-all-done = f32[2,3,192,192]{3,0,1,2:T(2,128)S(1)} async-done(((f32[2,3,192,192]{3,0,1,2:T(2,128)}), f32[2,3,192,192]{3,0,1,2:T(2,128)S(1)}, u32[]{:S(2)}, u32[]{:S(2)}) %all-to-all-start) | async-done | bytes 884768 | tf_op jit(solution)/shard_map/while/body/eval_jaxpr/all_to_all | solution.py:84
  259.8 3.0 fusion.83
  266.3 7.4 %all-to-all-start.1 = ((f32[2,192,3,192]{3,0,2,1:T(2,128)}), f32[2,192,3,192]{3,0,2,1:T(2,128)S(1)}, u32[]{:S(2)}, u32[]{:S(2)}) async-start(f32[2,192,3,192]{3,0,2,1:T(2,128)} %copy.46), calls=%async_computation.1 | async-start | bytes 2359296 | tf_op jit(solution)/shard_map/while/body/eval_jaxpr/all_to_all | solution.py:78
  273.8 31.2 %all-to-all-done.1 = f32[2,192,3,192]{3,0,2,1:T(2,128)S(1)} async-done(((f32[2,192,3,192]{3,0,2,1:T(2,128)}), f32[2,192,3,192]{3,0,2,1:T(2,128)S(1)}, u32[]{:S(2)}, u32[]{:S(2)}) %all-to-all-start.1) | async-done | bytes 884768 | tf_op jit(solution)/shard_map/while/body/eval_jaxpr/all_to_all | solution.py:78
  305.4 3.0 convolution_bitcast_fusion.9
  308.4 3.4 %fusion.84 = f32[2,3,192,192]{3,2,1,0:T(8,128)S(1)} fusion(f32[2,3,192,192]{2,3,1,0:T(8,128)S(1)} %convolution_bitcast_fusion.9, f32[2,3,192,192]{3,2,1,0:T(8,128)S(1)} %copy-done.4, f32[3,192,192]{2,1,0:T(8,128)S(1)} %copy-done.1, pred[]{:T(512)S(6)} %compare.14), kind=kOutput, calls=%fused_computation.4.clone.1 | convolution fusion | flops 510640128 | bytes 3096577 | tf_op jit(solution)/shard_map/while/body/eval_jaxpr/pxyz,zk->pxyk/dot_general | solution.py:38
  (52 shorter events, 16.3 us)
Async XLA Ops:
  6.5 1.3 copy-start
  7.8 0.7 copy-start.6
  8.5 0.7 copy-start.7
  9.1 50.4 %copy-start.2 = (f32[2,3,192,192]{3,2,1,0:T(8,128)}, f32[2,3,192,192]{3,2,1,0:T(8,128)S(1)}, u32[]{:S(2)}) copy-start(f32[2,3,192,192]{3,2,1,0:T(8,128)S(1)} %get-tuple-element.343) | copy-start | bytes 2654212 | tf_op jit(solution)/shard_map/while
  9.1 50.4 %all-reduce.2.cloned.1.call-start = ((), (), s32[]{:S(2)}) async-start(), calls=%async_computation.2 | async-start | bytes 1179648 | tf_op jit(solution)/shard_map/while/body/eval_jaxpr/psum | solution.py:14
  66.2 44.3 %all-to-all-start = ((f32[2,3,192,192]{3,0,1,2:T(2,128)}), f32[2,3,192,192]{3,0,1,2:T(2,128)S(1)}, u32[]{:S(2)}, u32[]{:S(2)}) async-start(f32[2,3,192,192]{3,0,1,2:T(2,128)} %copy.44), calls=%async_computation | async-start | bytes 2359296 | tf_op jit(solution)/shard_map/while/body/eval_jaxpr/all_to_all | solution.py:84
  117.5 38.6 %all-to-all-start.1 = ((f32[2,192,3,192]{3,0,2,1:T(2,128)}), f32[2,192,3,192]{3,0,2,1:T(2,128)S(1)}, u32[]{:S(2)}, u32[]{:S(2)}) async-start(f32[2,192,3,192]{3,0,2,1:T(2,128)} %copy.46), calls=%async_computation.1 | async-start | bytes 2359296 | tf_op jit(solution)/shard_map/while/body/eval_jaxpr/all_to_all | solution.py:78
  156.5 3.1 copy-start.1
  156.5 3.1 copy-start.4
  159.6 4.4 %copy-start.3 = (f32[2,3,192,192]{3,2,1,0:T(8,128)S(1)}, f32[2,3,192,192]{3,2,1,0:T(8,128)}, u32[]{:S(2)}) copy-start(f32[2,3,192,192]{3,2,1,0:T(8,128)} %copy-done.2) | copy-start | bytes 2654212 | tf_op jit(solution)/shard_map/while
  163.0 1.0 copy-start.5
  164.0 44.5 %copy-start.2 = (f32[2,3,192,192]{3,2,1,0:T(8,128)}, f32[2,3,192,192]{3,2,1,0:T(8,128)S(1)}, u32[]{:S(2)}) copy-start(f32[2,3,192,192]{3,2,1,0:T(8,128)S(1)} %get-tuple-element.343) | copy-start | bytes 2654212 | tf_op jit(solution)/shard_map/while
  164.0 44.5 %all-reduce.2.cloned.1.call-start = ((), (), s32[]{:S(2)}) async-start(), calls=%async_computation.2 | async-start | bytes 1179648 | tf_op jit(solution)/shard_map/while/body/eval_jaxpr/psum | solution.py:14
  215.1 44.3 %all-to-all-start = ((f32[2,3,192,192]{3,0,1,2:T(2,128)}), f32[2,3,192,192]{3,0,1,2:T(2,128)S(1)}, u32[]{:S(2)}, u32[]{:S(2)}) async-start(f32[2,3,192,192]{3,0,1,2:T(2,128)} %copy.44), calls=%async_computation | async-start | bytes 2359296 | tf_op jit(solution)/shard_map/while/body/eval_jaxpr/all_to_all | solution.py:84
  266.3 38.6 %all-to-all-start.1 = ((f32[2,192,3,192]{3,0,2,1:T(2,128)}), f32[2,192,3,192]{3,0,2,1:T(2,128)S(1)}, u32[]{:S(2)}, u32[]{:S(2)}) async-start(f32[2,192,3,192]{3,0,2,1:T(2,128)} %copy.46), calls=%async_computation.1 | async-start | bytes 2359296 | tf_op jit(solution)/shard_map/while/body/eval_jaxpr/all_to_all | solution.py:78
  305.3 3.1 copy-start.1
  305.3 3.1 copy-start.4
  308.4 4.4 %copy-start.3 = (f32[2,3,192,192]{3,2,1,0:T(8,128)S(1)}, f32[2,3,192,192]{3,2,1,0:T(8,128)}, u32[]{:S(2)}) copy-start(f32[2,3,192,192]{3,2,1,0:T(8,128)} %copy-done.2) | copy-start | bytes 2654212 | tf_op jit(solution)/shard_map/while
  311.8 1.0 copy-start.5
Sparse Core Ops, SparseCore 0:
  14.1 45.4 all-reduce.1
  168.9 39.4 all-reduce.1
where the time goes:
time: 322 us; the launch traced here: 320 us
  waiting for transfers between devices  211 us (66%)
  starting transfers between devices  39 us (12%)
  matrix products  32.8 us (10%)
  between operations  13.4 us (4%)
  local copies, waits for them, and re-layouts  12.8 us (4%)
  other arithmetic  5.52 us (2%)
  loops' own time  4.72 us (1%)
    psum x2, waiting for transfers between devices, broadcast(): return lax.psum(jnp.where(mine, x, jnp.zeros_like(x)), axis)  85.3 us
    all_to_all x2, waiting for transfers between devices, update(): lax.all_to_all(to_spectrum(density), 'slab', split_axis=2, concat_axis=1,...  63.8 us
    all_to_all x2, waiting for transfers between devices, back_each(): lax.all_to_all(convolve(pencil), 'slab', split_axis=1, concat_axis=2, til...  62.3 us
    all_to_all x2, starting transfers between devices, update(): lax.all_to_all(to_spectrum(density), 'slab', split_axis=2, concat_axis=1,...  24.2 us
    all_to_all x2, starting transfers between devices, back_each(): lax.all_to_all(convolve(pencil), 'slab', split_axis=1, concat_axis=2, til...  14.8 us
    dot_general x4, matrix products, along_z(): jnp.einsum('pxyz,zk->pxyk', values, matrix, precision=lax.Precision.HIGHEST)  13 us
    dot_general x4, matrix products, along_x(): jnp.einsum('pxyz,xk->pkyz', values, matrix, precision=lax.Precision.HIGHEST)  9.88 us
    dot_general x4, matrix products, along_y(): jnp.einsum('pxyz,yk->pxkz', values, matrix, precision=lax.Precision.HIGHEST)  9.88 us
  transfers between devices with their start and end apart: 6, of which 6 were waited for; matrix products, arithmetic and copies ran while one was open for 0% of the time, Pallas kernels for 0%

commit v1 on v0

v1 whole, which is shorter than its diff:
```python
import functools
import math

import jax
import jax.numpy as jnp
import numpy as np
from jax import lax
from jax.experimental import pallas as pl
from jax.experimental.pallas import tpu as pltpu
from jax.sharding import PartitionSpec as P

MESH = pl.DeviceIdType.MESH
F32, BF16 = jnp.float32, jnp.bfloat16
grid_step = 0.25
omega = 0.106
NG, SL, PL3, LN = 192, 64, 3, 128
ROWS, CUT = 56, 24


def split_host(matrix):
    high = matrix.astype(BF16)
    low = (matrix - high.astype(np.float64)).astype(BF16)
    return np.stack([np.asarray(high), np.asarray(low)])


def matrices():
    i = np.arange(NG)
    phase = 2.0 * np.pi / NG * ((i[:, None] * i[None, :]) % NG)
    cas = np.cos(phase) + np.sin(phase)
    first, second = np.zeros((256, 256)), np.zeros((256, 256))
    a, b, c = np.arange(128), np.arange(128, 192), np.arange(192, 256)
    pos0 = np.concatenate([a, b])
    pos1 = np.concatenate([a, c])
    first[np.ix_(pos0, pos0)] = cas
    second[np.ix_(pos1, pos1)] = cas
    order = (3 * np.arange(SL)[None, :] + np.arange(PL3)[:, None]).reshape(-1)
    across = cas[:, order]
    return [split_host(m) for m in (cas, np.stack([first, second]), across, across.T)]


def halves(v):
    high = v.astype(BF16)
    return high, (v - high.astype(F32)).astype(BF16)


def dot(a, b):
    return jnp.dot(a, b, preferred_element_type=F32)


def left(m_ref, v):
    high, low = halves(v)
    return dot(m_ref[0], high) + dot(m_ref[0], low) + dot(m_ref[1], high)


def along_z(b0, b1, b2, m_ref):
    (h0, l0), (h1, l1), (h2, l2) = halves(b0), halves(b1), halves(b2)

    def one(k, h, l):
        high, low = jnp.concatenate([h, h2], 1), jnp.concatenate([l, l2], 1)
        return dot(high, m_ref[0, k]) + dot(low, m_ref[0, k]) + dot(high, m_ref[1, k])

    r0, r1 = one(0, h0, l0), one(1, h1, l1)
    return r0[:, :LN], r1[:, :LN], r0[:, LN:] + r1[:, LN:]


def signed_square(mode):
    m = jnp.where(mode <= NG // 2, mode, mode - NG).astype(F32)
    wave = 2.0 * math.pi / (NG * grid_step) * m
    return wave * wave


def screened(squares):
    nonzero = jnp.where(squares > 0, squares, jnp.ones_like(squares))
    value = 4.0 * math.pi * (1.0 - jnp.exp(-squares / (4.0 * omega * omega))) / nonzero
    return jnp.where(squares > 0, value, jnp.full_like(squares, math.pi / (omega * omega)))


def kernel(
    occ_index, band_pick, bands, occupied, cas, zmat, xmat, xmat_t, out,
    send1, recv1, send2, recv2, own, got, part, cross, full, target, orb, table, acc,
    s1, r1, s2, r2, xs, xr,
):
    band, slab = lax.axis_index("band"), lax.axis_index("slab")
    y_lo, core = band // 2, band % 2
    zz, xy = slab // 8, slab % 8

    def peer(i):
        t, u = i % 8, i // 8
        dz = jnp.where(t % 2 == 1, (t + 1) // 2, 8 - t // 2)
        dxy = (u + t) % 8
        y, x = (xy // 4 + dxy // 4) % 2, (xy % 4 + dxy % 4) % 4
        return ((zz + dz) % 8) * 8 + y * 4 + x

    partner = {"band": y_lo * 2 + (1 - core)}
    across = {"band": (1 - y_lo) * 2 + core}
    barrier = pltpu.get_barrier_semaphore()

    def greet(i, carry):
        pl.semaphore_signal(barrier, inc=1, device_id={"slab": peer(i)}, device_id_type=MESH)
        return carry

    pl.semaphore_signal(barrier, inc=1, device_id=partner, device_id_type=MESH)
    pl.semaphore_signal(barrier, inc=1, device_id=across, device_id_type=MESH)
    lax.fori_loop(1, SL, greet, 0)

    for w in range(2):
        which = occ_index[w]
        mine = which // 4 == band
        for x in range(3):
            v = occupied[which % 4, x]
            v = jnp.where(mine, v, jnp.zeros_like(v))
            own[w, pl.ds(x * NG, NG), :] = v[:, :LN]
            high = v[:, LN:]
            own[w, pl.ds(576 + x * 96, 96), :] = jnp.concatenate([high[:96], high[96:]], 1)
    for x in range(3):
        t0, t1 = bands[band_pick[0], x], bands[band_pick[1], x]
        target[x, 0] = t0[:, :LN]
        target[x, 1] = t1[:, :LN]
        target[x, 2] = jnp.concatenate([t0[:, LN:], t1[:, LN:]], 1)

    pl.semaphore_wait(barrier, SL + 1)

    def hop(src, dst, k, where):
        return pltpu.make_async_remote_copy(
            src_ref=src, dst_ref=dst, send_sem=xs.at[k], recv_sem=xr.at[k], device_id=where, device_id_type=MESH
        )

    half = 432
    mine_rows = pl.ds(pl.multiple_of(core * half, 8), half)
    other_rows = pl.ds(pl.multiple_of((1 - core) * half, 8), half)
    first = [hop(own.at[w, other_rows], got.at[w], w, partner) for w in range(2)]
    second = [hop(part.at[w], cross.at[w], 2 + w, across) for w in range(2)]
    third = [hop(full.at[w, mine_rows], full.at[w, mine_rows], 4 + w, partner) for w in range(2)]
    first[0].start()
    first[1].start()
    for w in range(2):
        first[w].wait_recv()
        part[w] = own[w, mine_rows] + got[w]
        second[w].start()

    for j in range(3):
        ky = signed_square(jnp.full((NG, LN), j * SL, jnp.int32) + slab)
        kx = signed_square(lax.broadcasted_iota(jnp.int32, (NG, LN), 0))
        lane = lax.broadcasted_iota(jnp.int32, (NG, LN), 1)
        for b in range(2):
            kz = signed_square(lane if b == 0 else LN + lane % 64)
            table[j, b] = screened(kx + ky + kz) * (1.0 / float(NG * NG * NG))

    flat1, flat2 = send1.reshape(SL * ROWS, LN), send2.reshape(SL * ROWS, LN)
    in1, in2 = recv1.reshape(SL * ROWS, LN), recv2.reshape(SL * ROWS, LN)

    def rows_of(chunk):
        return pl.ds(0, CUT) if chunk == 0 else pl.ds(CUT, ROWS - CUT)

    def scatter(src, dst, ssem, rsem, chunk):
        rows = rows_of(chunk)

        def one(i, carry):
            d = peer(i)
            pltpu.make_async_remote_copy(
                src_ref=src.at[d, rows], dst_ref=dst.at[slab, rows], send_sem=ssem.at[chunk],
                recv_sem=rsem.at[chunk], device_id={"slab": d}, device_id_type=MESH,
            ).start()
            return carry

        lax.fori_loop(1, SL, one, 0)
        pltpu.make_async_copy(src.at[slab, rows], dst.at[slab, rows], rsem.at[chunk]).start()

    def arrived(dst, rsem, chunk):
        ref = dst.at[:, rows_of(chunk)]
        pltpu.make_async_copy(ref, ref, rsem.at[chunk]).wait()

    def sent(src, ssem, chunk):
        ref = src.at[pl.ds(0, SL - 1), rows_of(chunk)]
        pltpu.make_async_copy(ref, ref, ssem.at[chunk]).wait()

    low_lane = lax.broadcasted_iota(jnp.int32, (96, LN), 1) < 64
    for w in range(2):
        second[w].wait_recv()
        full[w, mine_rows] = part[w] + cross[w]
        third[w].start()
        third[w].wait_recv()
        for x in range(3):
            orb[w, x, 0] = full[w, pl.ds(x * NG, NG)]
            packed = full[w, pl.ds(576 + x * 96, 96)]
            turned = pltpu.roll(packed, 64, 1)
            orb[w, x, 1, :96] = jnp.where(low_lane, packed, turned)
            orb[w, x, 1, 96:] = jnp.where(low_lane, turned, packed)
        for x in range(3):
            o0, o1 = orb[w, x, 0], orb[w, x, 1]
            blocks = along_z(target[x, 0] * o0, target[x, 1] * o0, target[x, 2] * o1, zmat)
            for b in range(3):
                v = left(cas, blocks[b])
                for j in range(3):
                    n = w * 9 + j * 3 + b
                    flat1[pl.ds(n * 3 + x, SL, stride=ROWS), :] = v[j * SL : (j + 1) * SL]
        scatter(send1, recv1, s1, r1, w)

    for chunk in range(2):
        arrived(recv1, r1, chunk)
        for n in range(0, 8, 2) if chunk == 0 else range(8, 18, 2):
            cols = []
            for m in (n, n + 1):
                cols.append(jnp.concatenate([in1[pl.ds(m * 3 + x, SL, stride=ROWS), :] for x in range(3)], 0))
            v = left(xmat, jnp.concatenate(cols, 1))
            scale = [table[(m % 9) // 3, (m % 3) // 2] for m in (n, n + 1)]
            v = left(xmat_t, v * jnp.concatenate(scale, 1))
            for k, m in enumerate((n, n + 1)):
                for x in range(3):
                    flat2[pl.ds(m * 3 + x, SL, stride=ROWS), :] = v[x * SL : (x + 1) * SL, k * LN : (k + 1) * LN]
        scatter(send2, recv2, s2, r2, chunk)

    for chunk in range(2):
        arrived(recv2, r2, chunk)
    for x in range(3):
        for w in range(2):
            blocks = []
            for b in range(3):
                rows = [in2[pl.ds((w * 9 + j * 3 + b) * 3 + x, SL, stride=ROWS), :] for j in range(3)]
                blocks.append(left(cas, jnp.concatenate(rows, 0)))
            blocks = along_z(*blocks, zmat)
            o0, o1 = orb[w, x, 0], orb[w, x, 1]
            for b, o in enumerate((o0, o0, o1)):
                acc[b] = -blocks[b] * o if w == 0 else acc[b] - blocks[b] * o
        for p in range(2):
            out[p, x] = jnp.concatenate([acc[p], acc[2][:, p * 64 : (p + 1) * 64]], 1)

    for w in range(2):
        first[w].wait_send()
        second[w].wait_send()
        third[w].wait_send()
        sent(send1, s1, w)
        sent(send2, s2, w)


def shards(bands, occupied, occ_index, band_pick):
    vmem, smem = pl.BlockSpec(memory_space=pltpu.VMEM), pl.BlockSpec(memory_space=pltpu.SMEM)
    big = pltpu.VMEM((SL, ROWS, LN), F32)
    return pl.pallas_call(
        kernel,
        out_shape=jax.ShapeDtypeStruct((2, PL3, NG, NG), F32),
        in_specs=[smem, smem] + [vmem] * 6,
        out_specs=vmem,
        scratch_shapes=[
            big, big, big, big,
            pltpu.VMEM((2, 864, LN), F32),
            pltpu.VMEM((2, 432, LN), F32),
            pltpu.VMEM((2, 432, LN), F32),
            pltpu.VMEM((2, 432, LN), F32),
            pltpu.VMEM((2, 864, LN), F32),
            pltpu.VMEM((PL3, 3, NG, LN), F32),
            pltpu.VMEM((2, PL3, 2, NG, LN), F32),
            pltpu.VMEM((3, 2, NG, LN), F32),
            pltpu.VMEM((3, NG, LN), F32),
            pltpu.SemaphoreType.DMA((2,)),
            pltpu.SemaphoreType.DMA((2,)),
            pltpu.SemaphoreType.DMA((2,)),
            pltpu.SemaphoreType.DMA((2,)),
            pltpu.SemaphoreType.DMA((6,)),
            pltpu.SemaphoreType.DMA((6,)),
        ],
        compiler_params=pltpu.CompilerParams(
            collective_id=0, has_side_effects=True, vmem_limit_bytes=48 * 1024 * 1024
        ),
    )(occ_index, band_pick, bands, occupied, *(jnp.asarray(m) for m in matrices()))


def solution(mesh):
    placed = (P("band", "slab", None, None), P("band", "slab", None, None), P(), P("band"))
    return jax.shard_map(
        shards, mesh=mesh, in_specs=placed, out_specs=P("band", "slab", None, None), check_vma=False
    )
```

time: 322 us -> 122 us (0.38)
  waiting for transfers between devices: 211 us -> 0 us
  Pallas kernels: 0 us -> 111 us
  starting transfers between devices: 39 us -> 0 us
  matrix products: 32.8 us -> 0 us
  between operations: 13.4 us -> 0.02 us
  other arithmetic: 5.52 us -> 0 us
  loops' own time: 4.72 us -> 0 us
  local copies, waits for them, and re-layouts: 12.8 us -> 9.08 us
    all_to_all x4 -> x0, waiting for transfers between devices: 126 us -> none  [the longest x2 63.8 us: update(): lax.all_to_all(to_spectrum(density), 'slab', split_axis=2, concat_axis=1,...]
    pallas_call x0 -> x1, Pallas kernels: none -> 111 us  [shards(): pl.pallas_call(kernel, out_shape=jax.ShapeDtypeStruct((2, PL3, NG, NG), F...]
    psum x2 -> x0, waiting for transfers between devices: 85.3 us -> none  [broadcast(): return lax.psum(jnp.where(mine, x, jnp.zeros_like(x)), axis)]
    all_to_all x4 -> x0, starting transfers between devices: 39 us -> none  [the longest x2 24.2 us: update(): lax.all_to_all(to_spectrum(density), 'slab', split_axis=2, concat_axis=1,...]
    dot_general x12 -> x0, matrix products: 32.8 us -> none  [the longest x4 13 us: along_z(): jnp.einsum('pxyz,zk->pxyk', values, matrix, precision=lax.Precision.HIGHEST)]
    unnamed x6 -> x17, local copies, waits for them, and re-layouts: 0.85 us -> 9.08 us
    transpose x4 -> x0, local copies, waits for them, and re-layouts: 6.31 us -> none  [the longest x2 3.15 us: along_y(): jnp.einsum('pxyz,yk->pxkz', values, matrix, precision=lax.Precision.HIGHEST)]
    select_n x4 -> x0, other arithmetic: 4.82 us -> none  [the longest x2 3.9 us: broadcast(): return lax.psum(jnp.where(mine, x, jnp.zeros_like(x)), axis)]
  transfers between devices with their start and end apart: 6 -> 0, of which waited for: 6 -> 0; matrix products, arithmetic and copies ran while one was open for 0% -> 0% of each run, Pallas kernels for 0% -> 0%
where the time goes in v1:
time: 122 us; the launch traced here: 120 us
  Pallas kernels  111 us (91%)
  local copies, waits for them, and re-layouts  9.08 us (7%)
    pallas_call x1, Pallas kernels, shards(): pl.pallas_call(kernel, out_shape=jax.ShapeDtypeStruct((2, PL3, NG, NG), F...  111 us
    unnamed x17, local copies, waits for them, and re-layouts  9.08 us

profile of v1, /device:TPU:8, one launch (start us, length us, event | category | flops | bytes accessed | tf_op | source)
XLA Modules:
  0.0 119.9 jit_solution(8108341757943985523)
XLA Ops:
  0.0 0.0 copy-start
  0.0 1.7 %copy-done = f32[4,3,192,192]{3,2,1,0:T(8,128)S(1)} copy-done((f32[4,3,192,192]{3,2,1,0:T(8,128)S(1)}, f32[4,3,192,192]{3,2,1,0:T(8,128)}, u32[]{:S(2)}) %copy-start) | copy-done | bytes 1769496
  1.7 0.0 copy-start.1
  1.7 1.3 %copy-done.1 = f32[2,3,192,192]{3,2,1,0:T(8,128)S(1)} copy-done((f32[2,3,192,192]{3,2,1,0:T(8,128)S(1)}, f32[2,3,192,192]{3,2,1,0:T(8,128)}, u32[]{:S(2)}) %copy-start.1) | copy-done | bytes 884760
  2.9 0.0 copy-start.2
  2.9 1.0 copy-done.2
  4.0 0.0 copy-start.3
  4.0 0.9 copy-done.3
  4.9 0.0 copy-start.4
  4.9 0.9 copy-done.4
  5.8 0.0 copy-start.5
  5.8 0.9 copy-done.5
  6.8 0.0 copy-start.6
  6.8 0.7 copy-done.6
  7.4 0.0 copy-start.7
  7.4 0.7 copy-done.7
  8.1 110.9 %shard_map.82 = f32[2,3,192,192]{3,2,1,0:T(8,128)S(1)} custom-call(s32[2]{0:T(128)S(1)} %copy-done.6, s32[2]{0:T(128)S(1)} %copy-done.7, f32[2,3,192,192]{3,2,1,0:T(8,128)S(1)} %copy-done.1, f32[4,3,192,192]{3,2,1,0:T(8,128)S(1)} %copy-done, bf16[2,192,192]{2,1,0:T(8,128)(2,1)S(1)} %copy-done.5, bf16[2,2,256,256]{3,2,1,0:T(8,128)(2,1)S(1)} %copy-done.2, ...), custom_call_target="tpu_custom_call" | custom-call | tf_op jit(solution)/shard_map/pallas_call | solution.py:239
  118.9 1.0 copy.10
Async XLA Ops:
  0.0 1.7 %copy-start = (f32[4,3,192,192]{3,2,1,0:T(8,128)S(1)}, f32[4,3,192,192]{3,2,1,0:T(8,128)}, u32[]{:S(2)}) copy-start(f32[4,3,192,192]{3,2,1,0:T(8,128)} %occupied.1) | copy-start | bytes 5308420
  1.7 1.3 %copy-start.1 = (f32[2,3,192,192]{3,2,1,0:T(8,128)S(1)}, f32[2,3,192,192]{3,2,1,0:T(8,128)}, u32[]{:S(2)}) copy-start(f32[2,3,192,192]{3,2,1,0:T(8,128)} %bands.1) | copy-start | bytes 2654212
  2.9 1.0 copy-start.2
  4.0 0.9 copy-start.3
  4.9 0.9 copy-start.4
  5.8 0.9 copy-start.5
  6.8 0.7 copy-start.6
  7.4 0.7 copy-start.7

commit v2 on v1

v2 whole, which is shorter than its diff:
```python
import functools
import math

import jax
import jax.numpy as jnp
import numpy as np
from jax import lax
from jax.experimental import pallas as pl
from jax.experimental.pallas import tpu as pltpu
from jax.sharding import PartitionSpec as P

MESH = pl.DeviceIdType.MESH
F32, BF16 = jnp.float32, jnp.bfloat16
grid_step = 0.25
omega = 0.106
NG, SL, PL3, LN = 192, 64, 3, 128
ROWS = 56
CHUNKS = ((0, 24), (24, 16), (40, 16))
BLOCKS = (range(0, 8), range(8, 13), range(13, 18))
Z_STEPS = (1, 7, 2, 6, 3, 5, 4)
XY_STEPS = ((0, 1), (0, 3), (1, 0), (0, 2), (1, 1), (1, 3), (1, 2))


def row_of(n, x):
    return n * 3 + x + (1 if n >= 13 else 0)


def split_host(matrix):
    high = matrix.astype(BF16)
    low = (matrix - high.astype(np.float64)).astype(BF16)
    return np.stack([np.asarray(high), np.asarray(low)])


def matrices():
    i = np.arange(NG)
    phase = 2.0 * np.pi / NG * ((i[:, None] * i[None, :]) % NG)
    cas = np.cos(phase) + np.sin(phase)
    first, second = np.zeros((256, 256)), np.zeros((256, 256))
    a, b, c = np.arange(128), np.arange(128, 192), np.arange(192, 256)
    pos0 = np.concatenate([a, b])
    pos1 = np.concatenate([a, c])
    first[np.ix_(pos0, pos0)] = cas
    second[np.ix_(pos1, pos1)] = cas
    order = (3 * np.arange(SL)[None, :] + np.arange(PL3)[:, None]).reshape(-1)
    across = cas[:, order]
    return [split_host(m) for m in (cas, np.stack([first, second]), across, across.T)]


def halves(v):
    high = v.astype(BF16)
    return high, (v - high.astype(F32)).astype(BF16)


def dot(a, b):
    return jnp.dot(a, b, preferred_element_type=F32)


def left(m_ref, v):
    high, low = halves(v)
    return dot(m_ref[0], high) + dot(m_ref[0], low) + dot(m_ref[1], high)


def along_z(b0, b1, b2, m_ref):
    (h0, l0), (h1, l1), (h2, l2) = halves(b0), halves(b1), halves(b2)

    def one(k, h, l):
        high, low = jnp.concatenate([h, h2], 1), jnp.concatenate([l, l2], 1)
        return dot(high, m_ref[0, k]) + dot(low, m_ref[0, k]) + dot(high, m_ref[1, k])

    r0, r1 = one(0, h0, l0), one(1, h1, l1)
    return r0[:, :LN], r1[:, :LN], r0[:, LN:] + r1[:, LN:]


def signed_square(mode):
    m = jnp.where(mode <= NG // 2, mode, mode - NG).astype(F32)
    wave = 2.0 * math.pi / (NG * grid_step) * m
    return wave * wave


def screened(squares):
    nonzero = jnp.where(squares > 0, squares, jnp.ones_like(squares))
    value = 4.0 * math.pi * (1.0 - jnp.exp(-squares / (4.0 * omega * omega))) / nonzero
    return jnp.where(squares > 0, value, jnp.full_like(squares, math.pi / (omega * omega)))


def kernel(
    occ_index, band_pick, bands_in, occupied_in, cas_in, zmat_in, xmat_in, xmat_t_in, out,
    send1, mid1, recv1, send2, mid2, recv2, own, got, part, cross, full, target, orb, table, acc,
    bands, occupied, cas, zmat, xmat, xmat_t,
    load, s_sem, r_sem, xs, xr,
):
    band, slab = lax.axis_index("band"), lax.axis_index("slab")
    y_lo, core = band // 2, band % 2
    zz, xy = slab // 8, slab % 8
    pairs = (
        (occupied_in, occupied), (bands_in, bands), (cas_in, cas), (zmat_in, zmat), (xmat_in, xmat), (xmat_t_in, xmat_t)
    )
    loads = [pltpu.make_async_copy(src, dst, load.at[k]) for k, (src, dst) in enumerate(pairs)]
    for copy in loads:
        copy.start()

    z_peers = [(zz + d) % 8 for d in Z_STEPS]
    xy_peers = [((xy // 4 + dy) % 2) * 4 + (xy % 4 + dx) % 4 for dy, dx in XY_STEPS]
    partner = {"band": y_lo * 2 + (1 - core)}
    across = {"band": (1 - y_lo) * 2 + core}
    barrier = pltpu.get_barrier_semaphore()
    for where in [partner, across] + [{"slab": z * 8 + xy} for z in z_peers] + [{"slab": zz * 8 + p} for p in xy_peers]:
        pl.semaphore_signal(barrier, inc=1, device_id=where, device_id_type=MESH)

    def pack(w):
        which = occ_index[w]
        mine = which // 4 == band
        for x in range(3):
            v = occupied[which % 4, x]
            v = jnp.where(mine, v, jnp.zeros_like(v))
            own[w, x, :NG] = v[:, :LN]
            high = v[:, LN:]
            own[w, x, NG:] = jnp.concatenate([high[:96], high[96:]], 1)

    def hop(src, dst, k, where):
        return pltpu.make_async_remote_copy(
            src_ref=src, dst_ref=dst, send_sem=xs.at[k], recv_sem=xr.at[k], device_id=where, device_id_type=MESH
        )

    half = 144
    mine_rows = pl.ds(pl.multiple_of(core * half, 8), half)
    other_rows = pl.ds(pl.multiple_of((1 - core) * half, 8), half)
    units = [(w, x) for w in range(2) for x in range(3)]
    first = [hop(own.at[w, x, other_rows], got.at[w, x], w * 3 + x, partner) for w, x in units]
    second = [hop(part.at[w, x], cross.at[w, x], 6 + w * 3 + x, across) for w, x in units]
    third = [hop(full.at[w, x, mine_rows], full.at[w, x, mine_rows], 12 + w * 3 + x, partner) for w, x in units]

    loads[0].wait()
    pack(0)
    pl.semaphore_wait(barrier, 16)
    for k in range(3):
        first[k].start()
    pack(1)
    for k in range(3, 6):
        first[k].start()
    for k, (w, x) in enumerate(units):
        first[k].wait_recv()
        part[w, x] = own[w, x, mine_rows] + got[w, x]
        second[k].start()

    loads[1].wait()
    for x in range(3):
        t0, t1 = bands[band_pick[0], x], bands[band_pick[1], x]
        target[x, 0] = t0[:, :LN]
        target[x, 1] = t1[:, :LN]
        target[x, 2] = jnp.concatenate([t0[:, LN:], t1[:, LN:]], 1)
    for copy in loads[2:]:
        copy.wait()

    for j in range(3):
        ky = signed_square(jnp.full((NG, LN), j * SL, jnp.int32) + slab)
        kx = signed_square(lax.broadcasted_iota(jnp.int32, (NG, LN), 0))
        lane = lax.broadcasted_iota(jnp.int32, (NG, LN), 1)
        for b in range(2):
            kz = signed_square(lane if b == 0 else LN + lane % 64)
            table[j, b] = screened(kx + ky + kz) * (1.0 / float(NG * NG * NG))

    flat1, in1, flat2, in2 = (r.reshape(SL * ROWS, LN) for r in (send1, recv1, send2, recv2))

    def exchange(src, dst, phase, chunk, along_zz):
        rows = pl.ds(*CHUNKS[chunk])
        k = phase * 3 + chunk
        for p in z_peers if along_zz else xy_peers:
            pltpu.make_async_remote_copy(
                src_ref=src.at[p, :, rows] if along_zz else src.at[:, p, rows],
                dst_ref=dst.at[zz, :, rows] if along_zz else dst.at[:, xy, rows],
                send_sem=s_sem.at[k], recv_sem=r_sem.at[k],
                device_id={"slab": p * 8 + xy if along_zz else zz * 8 + p}, device_id_type=MESH,
            ).start()
        if along_zz:
            pltpu.make_async_copy(src.at[zz, :, rows], dst.at[zz, :, rows], r_sem.at[k]).start()
        else:
            pltpu.make_async_copy(src.at[:, xy, rows], dst.at[:, xy, rows], r_sem.at[k]).start()

    def arrived(dst, phase, chunk):
        ref = dst.at[:, :, pl.ds(*CHUNKS[chunk])]
        pltpu.make_async_copy(ref, ref, r_sem.at[phase * 3 + chunk]).wait()

    def sent(src, phase, chunk):
        ref = src.at[pl.ds(0, 7), :, pl.ds(*CHUNKS[chunk])]
        pltpu.make_async_copy(ref, ref, s_sem.at[phase * 3 + chunk]).wait()

    low_lane = lax.broadcasted_iota(jnp.int32, (96, LN), 1) < 64

    def join(k):
        w, x = units[k]
        second[k].wait_recv()
        full[w, x, mine_rows] = part[w, x] + cross[w, x]
        third[k].start()

    def forward(k):
        w, x = units[k]
        third[k].wait_recv()
        orb[w, x, 0] = full[w, x, :NG]
        packed = full[w, x, NG:]
        turned = pltpu.roll(packed, 64, 1)
        orb[w, x, 1, :96] = jnp.where(low_lane, packed, turned)
        orb[w, x, 1, 96:] = jnp.where(low_lane, turned, packed)
        o0, o1 = orb[w, x, 0], orb[w, x, 1]
        blocks = along_z(target[x, 0] * o0, target[x, 1] * o0, target[x, 2] * o1, zmat)
        for b in range(3):
            v = left(cas, blocks[b])
            for j in range(3):
                flat1[pl.ds(row_of(w * 9 + j * 3 + b, x), SL, stride=ROWS), :] = v[j * SL : (j + 1) * SL]

    def middle(chunk):
        blocks = list(BLOCKS[chunk])
        for group in [blocks[i : i + 2] for i in range(0, len(blocks), 2)]:
            cols = [
                jnp.concatenate([in1[pl.ds(row_of(n, x), SL, stride=ROWS), :] for x in range(3)], 0) for n in group
            ]
            scale = [table[(n % 9) // 3, (n % 3) // 2] for n in group]
            v = left(xmat, jnp.concatenate(cols, 1))
            v = left(xmat_t, v * jnp.concatenate(scale, 1))
            for k, n in enumerate(group):
                for x in range(3):
                    flat2[pl.ds(row_of(n, x), SL, stride=ROWS), :] = v[x * SL : (x + 1) * SL, k * LN : (k + 1) * LN]

    def finish(w, x):
        blocks = []
        for b in range(3):
            rows = [in2[pl.ds(row_of(w * 9 + j * 3 + b, x), SL, stride=ROWS), :] for j in range(3)]
            blocks.append(left(cas, jnp.concatenate(rows, 0)))
        blocks = along_z(*blocks, zmat)
        o0, o1 = orb[w, x, 0], orb[w, x, 1]
        for b, o in enumerate((o0, o0, o1)):
            acc[x, b] = -blocks[b] * o if w == 0 else acc[x, b] - blocks[b] * o

    join(0)
    for k in range(6):
        if k < 5:
            join(k + 1)
        forward(k)
        if k == 2:
            exchange(send1, mid1, 0, 0, True)
    exchange(send1, mid1, 0, 1, True)
    exchange(send1, mid1, 0, 2, True)

    def relay1(chunk):
        arrived(mid1, 0, chunk)
        exchange(mid1, recv1, 1, chunk, False)

    def conv(chunk):
        arrived(recv1, 1, chunk)
        middle(chunk)
        exchange(send2, mid2, 2, chunk, False)

    def relay2(chunk):
        arrived(mid2, 2, chunk)
        exchange(mid2, recv2, 3, chunk, True)

    relay1(0)
    conv(0)
    relay1(1)
    conv(1)
    relay2(0)
    relay1(2)
    relay2(1)
    conv(2)
    relay2(2)
    arrived(recv2, 3, 0)
    arrived(recv2, 3, 1)
    for x in range(3):
        finish(0, x)
    arrived(recv2, 3, 2)
    for x in range(3):
        finish(1, x)
        for p in range(2):
            out[p, x] = jnp.concatenate([acc[x, p], acc[x, 2][:, p * 64 : (p + 1) * 64]], 1)

    for k in range(6):
        first[k].wait_send()
        second[k].wait_send()
        third[k].wait_send()
    for phase, src in enumerate((send1, mid1, send2, mid2)):
        for chunk in range(3):
            sent(src, phase, chunk)


def shards(bands, occupied, occ_index, band_pick):
    vmem, smem = pl.BlockSpec(memory_space=pltpu.VMEM), pl.BlockSpec(memory_space=pltpu.SMEM)
    constants = [jnp.asarray(m) for m in matrices()]
    arrays = [occupied, bands] + constants
    big = pltpu.VMEM((8, 8, ROWS, LN), F32)
    return pl.pallas_call(
        kernel,
        out_shape=jax.ShapeDtypeStruct((2, PL3, NG, NG), F32),
        in_specs=[smem, smem] + [pl.BlockSpec(memory_space=pl.ANY)] * 6,
        out_specs=vmem,
        scratch_shapes=[
            big, big, big, big, big, big,
            pltpu.VMEM((2, 3, 288, LN), F32),
            pltpu.VMEM((2, 3, 144, LN), F32),
            pltpu.VMEM((2, 3, 144, LN), F32),
            pltpu.VMEM((2, 3, 144, LN), F32),
            pltpu.VMEM((2, 3, 288, LN), F32),
            pltpu.VMEM((PL3, 3, NG, LN), F32),
            pltpu.VMEM((2, PL3, 2, NG, LN), F32),
            pltpu.VMEM((3, 2, NG, LN), F32),
            pltpu.VMEM((3, 3, NG, LN), F32),
            pltpu.VMEM(bands.shape, F32),
            pltpu.VMEM(occupied.shape, F32),
            *(pltpu.VMEM(m.shape, BF16) for m in constants),
            pltpu.SemaphoreType.DMA((6,)),
            pltpu.SemaphoreType.DMA((12,)),
            pltpu.SemaphoreType.DMA((12,)),
            pltpu.SemaphoreType.DMA((18,)),
            pltpu.SemaphoreType.DMA((18,)),
        ],
        compiler_params=pltpu.CompilerParams(
            collective_id=0, has_side_effects=True, vmem_limit_bytes=62 * 1024 * 1024
        ),
    )(occ_index, band_pick, bands, occupied, *constants)


def solution(mesh):
    placed = (P("band", "slab", None, None), P("band", "slab", None, None), P(), P("band"))
    return jax.shard_map(
        shards, mesh=mesh, in_specs=placed, out_specs=P("band", "slab", None, None), check_vma=False
    )
```

time: 122 us -> 119 us (0.975)
  local copies, waits for them, and re-layouts: 9.08 us -> 2.42 us
  Pallas kernels: 111 us -> 115 us
    unnamed x17 -> x1, local copies, waits for them, and re-layouts: 9.08 us -> 2.42 us
    pallas_call x1, Pallas kernels: 111 us -> 115 us  [shards(): pl.pallas_call(kernel, out_shape=jax.ShapeDtypeStruct((2, PL3, NG, NG), F...]
where the time goes in v2:
time: 119 us; the launch traced here: 117 us
  Pallas kernels  115 us (97%)
  local copies, waits for them, and re-layouts  2.42 us (2%)
    pallas_call x1, Pallas kernels, shards(): pl.pallas_call(kernel, out_shape=jax.ShapeDtypeStruct((2, PL3, NG, NG), F...  115 us
    unnamed x1, local copies, waits for them, and re-layouts  2.42 us

profile of v2, /device:TPU:8, one launch (start us, length us, event | category | flops | bytes accessed | tf_op | source)
XLA Modules:
  0.0 117.3 jit_solution(18365974189185250134)
XLA Ops:
  0.0 114.9 %shard_map.82 = f32[2,3,192,192]{3,2,1,0:T(8,128)} custom-call(s32[2]{0:T(128)} %occ_index.1, s32[2]{0:T(128)} %band_pick.1, f32[2,3,192,192]{3,2,1,0:T(8,128)} %bands_in.1, f32[4,3,192,192]{3,2,1,0:T(8,128)} %occupied_in.1, bf16[2,192,192]{2,1,0:T(8,128)(2,1)} %constant.8.clone.cas_in, bf16[2,2,256,256]{3,2,1,0:T(8,128)(2,1)} %constant.9.clone.zmat_in, ...), custom_call_target="tpu_custom_call" | custom-call | tf_op jit(solution)/shard_map/pallas_call | solution.py:290
  114.9 2.4 %copy.10 = f32[2,3,192,192]{3,2,1,0:T(8,128)} copy(f32[2,3,192,192]{3,2,1,0:T(8,128)} %shard_map.82) | data formatting | bytes 1769472

commit v3 on v2

--- a/solution.py
+++ b/solution.py
@@ -18,7 +18,7 @@
 CHUNKS = ((0, 24), (24, 16), (40, 16))
 BLOCKS = (range(0, 8), range(8, 13), range(13, 18))
 Z_STEPS = (1, 7, 2, 6, 3, 5, 4)
-XY_STEPS = ((0, 1), (0, 3), (1, 0), (0, 2), (1, 1), (1, 3), (1, 2))
+XY_STEPS = ((0, 1), (1, 3), (0, 0), (1, 0), (0, 3), (1, 1), (0, 2), (1, 2))
 
 
 def row_of(n, x):
@@ -104,7 +104,7 @@
     partner = {"band": y_lo * 2 + (1 - core)}
     across = {"band": (1 - y_lo) * 2 + core}
     barrier = pltpu.get_barrier_semaphore()
-    for where in [partner, across] + [{"slab": z * 8 + xy} for z in z_peers] + [{"slab": zz * 8 + p} for p in xy_peers]:
+    for where in [partner] + [{"slab": z * 8 + xy} for z in z_peers] + [{**across, "slab": zz * 8 + p} for p in xy_peers]:
         pl.semaphore_signal(barrier, inc=1, device_id=where, device_id_type=MESH)
 
     def pack(w):
@@ -170,19 +170,17 @@
                 src_ref=src.at[p, :, rows] if along_zz else src.at[:, p, rows],
                 dst_ref=dst.at[zz, :, rows] if along_zz else dst.at[:, xy, rows],
                 send_sem=s_sem.at[k], recv_sem=r_sem.at[k],
-                device_id={"slab": p * 8 + xy if along_zz else zz * 8 + p}, device_id_type=MESH,
+                device_id={"slab": p * 8 + xy} if along_zz else {**across, "slab": zz * 8 + p}, device_id_type=MESH,
             ).start()
         if along_zz:
             pltpu.make_async_copy(src.at[zz, :, rows], dst.at[zz, :, rows], r_sem.at[k]).start()
-        else:
-            pltpu.make_async_copy(src.at[:, xy, rows], dst.at[:, xy, rows], r_sem.at[k]).start()
 
     def arrived(dst, phase, chunk):
         ref = dst.at[:, :, pl.ds(*CHUNKS[chunk])]
         pltpu.make_async_copy(ref, ref, r_sem.at[phase * 3 + chunk]).wait()
 
     def sent(src, phase, chunk):
-        ref = src.at[pl.ds(0, 7), :, pl.ds(*CHUNKS[chunk])]
+        ref = src.at[pl.ds(0, 7 if phase % 3 == 0 else 8), :, pl.ds(*CHUNKS[chunk])]
         pltpu.make_async_copy(ref, ref, s_sem.at[phase * 3 + chunk]).wait()
 
     low_lane = lax.broadcasted_iota(jnp.int32, (96, LN), 1) < 64

time: 119 us -> 119 us (level); the launches traced: 117 us -> 119 us
    pallas_call x1, Pallas kernels: 115 us -> 116 us  [shards(): pl.pallas_call(kernel, out_shape=jax.ShapeDtypeStruct((2, PL3, NG, NG), F...]
where the time goes in v3:
time: 119 us
  Pallas kernels  116 us (97%)
  local copies, waits for them, and re-layouts  2.42 us (2%)
    pallas_call x1, Pallas kernels, shards(): pl.pallas_call(kernel, out_shape=jax.ShapeDtypeStruct((2, PL3, NG, NG), F...  116 us
    unnamed x1, local copies, waits for them, and re-layouts  2.42 us

profile of v3, /device:TPU:8, one launch (start us, length us, event | category | flops | bytes accessed | tf_op | source)
XLA Modules:
  0.0 118.9 jit_solution(15845201877459897970)
XLA Ops:
  0.0 116.5 %shard_map.82 = f32[2,3,192,192]{3,2,1,0:T(8,128)} custom-call(s32[2]{0:T(128)} %occ_index.1, s32[2]{0:T(128)} %band_pick.1, f32[2,3,192,192]{3,2,1,0:T(8,128)} %bands_in.1, f32[4,3,192,192]{3,2,1,0:T(8,128)} %occupied_in.1, bf16[2,192,192]{2,1,0:T(8,128)(2,1)} %constant.8.clone.cas_in, bf16[2,2,256,256]{3,2,1,0:T(8,128)(2,1)} %constant.9.clone.zmat_in, ...), custom_call_target="tpu_custom_call" | custom-call | tf_op jit(solution)/shard_map/pallas_call | solution.py:288
  116.5 2.4 %copy.10 = f32[2,3,192,192]{3,2,1,0:T(8,128)} copy(f32[2,3,192,192]{3,2,1,0:T(8,128)} %shard_map.82) | data formatting | bytes 1769472

commit v4 on v3

--- a/solution.py
+++ b/solution.py
@@ -236,8 +236,6 @@
         forward(k)
         if k == 2:
             exchange(send1, mid1, 0, 0, True)
-    exchange(send1, mid1, 0, 1, True)
-    exchange(send1, mid1, 0, 2, True)
 
     def relay1(chunk):
         arrived(mid1, 0, chunk)
@@ -252,14 +250,19 @@
         arrived(mid2, 2, chunk)
         exchange(mid2, recv2, 3, chunk, True)
 
+    sent(send1, 0, 0)
+    exchange(send1, mid1, 0, 1, True)
     relay1(0)
     conv(0)
+    sent(send1, 0, 1)
+    exchange(send1, mid1, 0, 2, True)
     relay1(1)
     conv(1)
+    sent(send1, 0, 2)
     relay2(0)
     relay1(2)
+    conv(2)
     relay2(1)
-    conv(2)
     relay2(2)
     arrived(recv2, 3, 0)
     arrived(recv2, 3, 1)
@@ -275,7 +278,7 @@
         first[k].wait_send()
         second[k].wait_send()
         third[k].wait_send()
-    for phase, src in enumerate((send1, mid1, send2, mid2)):
+    for phase, src in ((1, mid1), (2, send2), (3, mid2)):
         for chunk in range(3):
             sent(src, phase, chunk)
 

time: 119 us -> 119 us (level); the launches traced: 119 us -> 117 us
    pallas_call x1, Pallas kernels: 116 us -> 115 us  [shards(): pl.pallas_call(kernel, out_shape=jax.ShapeDtypeStruct((2, PL3, NG, NG), F...]
where the time goes in v4:
time: 119 us; the launch traced here: 117 us
  Pallas kernels  115 us (97%)
  local copies, waits for them, and re-layouts  2.42 us (2%)
    pallas_call x1, Pallas kernels, shards(): pl.pallas_call(kernel, out_shape=jax.ShapeDtypeStruct((2, PL3, NG, NG), F...  115 us
    unnamed x1, local copies, waits for them, and re-layouts  2.42 us

profile of v4, /device:TPU:8, one launch (start us, length us, event | category | flops | bytes accessed | tf_op | source)
XLA Modules:
  0.0 117.3 jit_solution(17863579259416057786)
XLA Ops:
  0.0 114.8 %shard_map.82 = f32[2,3,192,192]{3,2,1,0:T(8,128)} custom-call(s32[2]{0:T(128)} %occ_index.1, s32[2]{0:T(128)} %band_pick.1, f32[2,3,192,192]{3,2,1,0:T(8,128)} %bands_in.1, f32[4,3,192,192]{3,2,1,0:T(8,128)} %occupied_in.1, bf16[2,192,192]{2,1,0:T(8,128)(2,1)} %constant.8.clone.cas_in, bf16[2,2,256,256]{3,2,1,0:T(8,128)(2,1)} %constant.9.clone.zmat_in, ...), custom_call_target="tpu_custom_call" | custom-call | tf_op jit(solution)/shard_map/pallas_call | solution.py:291
  114.8 2.4 %copy.10 = f32[2,3,192,192]{3,2,1,0:T(8,128)} copy(f32[2,3,192,192]{3,2,1,0:T(8,128)} %shard_map.82) | data formatting | bytes 1769472

commit v5 on v3

--- a/solution.py
+++ b/solution.py
@@ -17,12 +17,14 @@
 ROWS = 56
 CHUNKS = ((0, 24), (24, 16), (40, 16))
 BLOCKS = (range(0, 8), range(8, 13), range(13, 18))
+WIDE = 58
 Z_STEPS = (1, 7, 2, 6, 3, 5, 4)
-XY_STEPS = ((0, 1), (1, 3), (0, 0), (1, 0), (0, 3), (1, 1), (0, 2), (1, 2))
 
 
 def row_of(n, x):
-    return n * 3 + x + (1 if n >= 13 else 0)
+    if n < 8:
+        return x * 8 + n
+    return 24 + x * 5 + n - 8 if n < 13 else 40 + x * 5 + n - 13
 
 
 def split_host(matrix):
@@ -41,9 +43,13 @@
     pos1 = np.concatenate([a, c])
     first[np.ix_(pos0, pos0)] = cas
     second[np.ix_(pos1, pos1)] = cas
-    order = (3 * np.arange(SL)[None, :] + np.arange(PL3)[:, None]).reshape(-1)
-    across = cas[:, order]
-    return [split_host(m) for m in (cas, np.stack([first, second]), across, across.T)]
+    slot = np.arange(SL)
+    rows, across = [], []
+    for x in range(4):
+        device = slot // 4 * 4 + (x + slot % 4 - 1) % 4
+        rows.append(split_host(cas[(np.arange(3)[:, None] * SL + device[None, :]).reshape(-1)]))
+        across.append(split_host(cas[:, (3 * device[None, :] + np.arange(PL3)[:, None]).reshape(-1)]))
+    return [np.stack(rows), split_host(np.stack([first, second])), np.stack(across)]
 
 
 def halves(v):
@@ -84,27 +90,36 @@
 
 
 def kernel(
-    occ_index, band_pick, bands_in, occupied_in, cas_in, zmat_in, xmat_in, xmat_t_in, out,
+    occ_index, band_pick, bands_in, occupied_in, rows_in, zmat_in, xmat_in, out,
     send1, mid1, recv1, send2, mid2, recv2, own, got, part, cross, full, target, orb, table, acc,
-    bands, occupied, cas, zmat, xmat, xmat_t,
+    bands, occupied, cas, zmat, xmat, cas_t, xmat_t,
     load, s_sem, r_sem, xs, xr,
 ):
     band, slab = lax.axis_index("band"), lax.axis_index("slab")
     y_lo, core = band // 2, band % 2
     zz, xy = slab // 8, slab % 8
+    yh, xx = xy // 4, xy % 4
     pairs = (
-        (occupied_in, occupied), (bands_in, bands), (cas_in, cas), (zmat_in, zmat), (xmat_in, xmat), (xmat_t_in, xmat_t)
+        (occupied_in, occupied), (bands_in, bands), (rows_in.at[xx], cas), (zmat_in, zmat), (xmat_in.at[xx], xmat)
     )
     loads = [pltpu.make_async_copy(src, dst, load.at[k]) for k, (src, dst) in enumerate(pairs)]
     for copy in loads:
         copy.start()
 
     z_peers = [(zz + d) % 8 for d in Z_STEPS]
-    xy_peers = [((xy // 4 + dy) % 2) * 4 + (xy % 4 + dx) % 4 for dy, dx in XY_STEPS]
+    up, down = (xx + 1) % 4, (xx + 3) % 4
+    turn = (xx + 1 + 2 * yh) % 4
     partner = {"band": y_lo * 2 + (1 - core)}
     across = {"band": (1 - y_lo) * 2 + core}
+
+    def at(z, y, x, **more):
+        return {"slab": z * 8 + y * 4 + x, **more}
+
+    greeted = [partner] + [at(z, yh, xx) for z in z_peers]
+    greeted += [at(z, yh, x) for z in [zz] + z_peers for x in (up, down)]
+    greeted += [at(zz, y, x, **across) for y in (0, 1) for x in (down, xx, up)]
     barrier = pltpu.get_barrier_semaphore()
-    for where in [partner] + [{"slab": z * 8 + xy} for z in z_peers] + [{**across, "slab": zz * 8 + p} for p in xy_peers]:
+    for where in greeted:
         pl.semaphore_signal(barrier, inc=1, device_id=where, device_id_type=MESH)
 
     def pack(w):
@@ -132,7 +147,7 @@
 
     loads[0].wait()
     pack(0)
-    pl.semaphore_wait(barrier, 16)
+    pl.semaphore_wait(barrier, len(greeted))
     for k in range(3):
         first[k].start()
     pack(1)
@@ -151,6 +166,9 @@
         target[x, 2] = jnp.concatenate([t0[:, LN:], t1[:, LN:]], 1)
     for copy in loads[2:]:
         copy.wait()
+    for h in range(2):
+        cas_t[h] = cas[h].astype(F32).T.astype(BF16)
+        xmat_t[h] = xmat[h].astype(F32).T.astype(BF16)
 
     for j in range(3):
         ky = signed_square(jnp.full((NG, LN), j * SL, jnp.int32) + slab)
@@ -162,25 +180,55 @@
 
     flat1, in1, flat2, in2 = (r.reshape(SL * ROWS, LN) for r in (send1, recv1, send2, recv2))
 
-    def exchange(src, dst, phase, chunk, along_zz):
-        rows = pl.ds(*CHUNKS[chunk])
-        k = phase * 3 + chunk
-        for p in z_peers if along_zz else xy_peers:
-            pltpu.make_async_remote_copy(
-                src_ref=src.at[p, :, rows] if along_zz else src.at[:, p, rows],
-                dst_ref=dst.at[zz, :, rows] if along_zz else dst.at[:, xy, rows],
-                send_sem=s_sem.at[k], recv_sem=r_sem.at[k],
-                device_id={"slab": p * 8 + xy} if along_zz else {**across, "slab": zz * 8 + p}, device_id_type=MESH,
-            ).start()
-        if along_zz:
-            pltpu.make_async_copy(src.at[zz, :, rows], dst.at[zz, :, rows], r_sem.at[k]).start()
-
-    def arrived(dst, phase, chunk):
-        ref = dst.at[:, :, pl.ds(*CHUNKS[chunk])]
+    def push(src, dst, k, where):
+        pltpu.make_async_remote_copy(
+            src_ref=src, dst_ref=dst, send_sem=s_sem.at[k], recv_sem=r_sem.at[k], device_id=where, device_id_type=MESH
+        ).start()
+
+    near = pl.ds(0, 3)
+
+    def forth_z(chunk, rows):
+        for z in z_peers:
+            push(send1.at[z, :, near, rows], mid1.at[zz, :, near, rows], chunk, at(z, yh, xx))
+            push(send1.at[z, 0, 3, rows], mid1.at[zz, 0, 3, rows], chunk, at(z, yh, up))
+            push(send1.at[z, 1, 3, rows], mid1.at[zz, 1, 3, rows], chunk, at(z, yh, down))
+        push(send1.at[zz, 0, 3, rows], mid1.at[zz, 0, 3, rows], chunk, at(zz, yh, up))
+        push(send1.at[zz, 1, 3, rows], mid1.at[zz, 1, 3, rows], chunk, at(zz, yh, down))
+        pltpu.make_async_copy(
+            send1.at[zz, :, near, rows], mid1.at[zz, :, near, rows], r_sem.at[chunk]
+        ).start()
+
+    def forth_xy(chunk):
+        rows, k = pl.ds(*CHUNKS[chunk]), 3 + chunk
+        for r, x in ((0, down), (2, up), (1, xx)):
+            for y in range(2):
+                push(mid1.at[:, y, r, rows], recv1.at[:, yh, 2 - r, rows], k, at(zz, y, x, **across))
+        push(mid1.at[:, 0, 3, rows], recv1.at[:, yh, 3, rows], k, at(zz, 0, up, **across))
+        push(mid1.at[:, 1, 3, rows], recv1.at[:, yh, 3, rows], k, at(zz, 1, down, **across))
+
+    def back_xy(chunk):
+        rows, k = pl.ds(*CHUNKS[chunk]), 6 + chunk
+        for r, x in ((0, down), (2, up), (1, xx)):
+            for y in range(2):
+                push(send2.at[:, y, r, rows], mid2.at[:, yh, 2 - r, rows], k, at(zz, y, x, **across))
+        push(send2.at[:, 0, 3, rows], mid2.at[:, yh, 3, rows], k, at(zz, 0, up, **across))
+        push(send2.at[:, 1, 3, rows], mid2.at[:, yh, 3, rows], k, at(zz, 1, down, **across))
+
+    def back_z(chunk):
+        rows, k = pl.ds(*CHUNKS[chunk]), 9 + chunk
+        for z in z_peers:
+            push(mid2.at[z, :, near, rows], recv2.at[zz, :, near, rows], k, at(z, yh, xx))
+            push(mid2.at[z, :, 3, rows], recv2.at[zz, :, 3, rows], k, at(z, yh, turn))
+        push(mid2.at[zz, :, 3, rows], recv2.at[zz, :, 3, rows], k, at(zz, yh, turn))
+        pltpu.make_async_copy(mid2.at[zz, :, near, rows], recv2.at[zz, :, near, rows], r_sem.at[k]).start()
+
+    def arrived(phase, chunk):
+        ref = (mid1, recv1, mid2, recv2)[phase].at[:, :, :, pl.ds(*CHUNKS[chunk])]
         pltpu.make_async_copy(ref, ref, r_sem.at[phase * 3 + chunk]).wait()
 
-    def sent(src, phase, chunk):
-        ref = src.at[pl.ds(0, 7 if phase % 3 == 0 else 8), :, pl.ds(*CHUNKS[chunk])]
+    def sent(phase, chunk):
+        ref = (send1, mid1, send2, mid2)[phase].reshape(SL, ROWS, LN)
+        ref = ref.at[pl.ds(0, WIDE if phase % 3 == 0 else SL), pl.ds(*CHUNKS[chunk])]
         pltpu.make_async_copy(ref, ref, s_sem.at[phase * 3 + chunk]).wait()
 
     low_lane = lax.broadcasted_iota(jnp.int32, (96, LN), 1) < 64
@@ -223,7 +271,7 @@
         blocks = []
         for b in range(3):
             rows = [in2[pl.ds(row_of(w * 9 + j * 3 + b, x), SL, stride=ROWS), :] for j in range(3)]
-            blocks.append(left(cas, jnp.concatenate(rows, 0)))
+            blocks.append(left(cas_t, jnp.concatenate(rows, 0)))
         blocks = along_z(*blocks, zmat)
         o0, o1 = orb[w, x, 0], orb[w, x, 1]
         for b, o in enumerate((o0, o0, o1)):
@@ -234,38 +282,38 @@
         if k < 5:
             join(k + 1)
         forward(k)
-        if k == 2:
-            exchange(send1, mid1, 0, 0, True)
-    exchange(send1, mid1, 0, 1, True)
-    exchange(send1, mid1, 0, 2, True)
-
-    def relay1(chunk):
-        arrived(mid1, 0, chunk)
-        exchange(mid1, recv1, 1, chunk, False)
+        if k < 3:
+            forth_z(0, pl.ds(8 * k, 8))
 
     def conv(chunk):
-        arrived(recv1, 1, chunk)
+        arrived(1, chunk)
         middle(chunk)
-        exchange(send2, mid2, 2, chunk, False)
-
-    def relay2(chunk):
-        arrived(mid2, 2, chunk)
-        exchange(mid2, recv2, 3, chunk, True)
-
-    relay1(0)
+        back_xy(chunk)
+
+    sent(0, 0)
+    forth_z(1, pl.ds(*CHUNKS[1]))
+    arrived(0, 0)
+    forth_xy(0)
     conv(0)
-    relay1(1)
+    sent(0, 1)
+    forth_z(2, pl.ds(*CHUNKS[2]))
+    arrived(2, 0)
+    back_z(0)
+    arrived(0, 1)
+    forth_xy(1)
+    arrived(0, 2)
+    forth_xy(2)
     conv(1)
-    relay2(0)
-    relay1(2)
-    relay2(1)
     conv(2)
-    relay2(2)
-    arrived(recv2, 3, 0)
-    arrived(recv2, 3, 1)
+    arrived(2, 1)
+    back_z(1)
+    arrived(2, 2)
+    back_z(2)
+    arrived(3, 0)
+    arrived(3, 1)
     for x in range(3):
         finish(0, x)
-    arrived(recv2, 3, 2)
+    arrived(3, 2)
     for x in range(3):
         finish(1, x)
         for p in range(2):
@@ -275,20 +323,21 @@
         first[k].wait_send()
         second[k].wait_send()
         third[k].wait_send()
-    for phase, src in enumerate((send1, mid1, send2, mid2)):
+    sent(0, 2)
+    for phase in range(1, 4):
         for chunk in range(3):
-            sent(src, phase, chunk)
+            sent(phase, chunk)
 
 
 def shards(bands, occupied, occ_index, band_pick):
     vmem, smem = pl.BlockSpec(memory_space=pltpu.VMEM), pl.BlockSpec(memory_space=pltpu.SMEM)
     constants = [jnp.asarray(m) for m in matrices()]
     arrays = [occupied, bands] + constants
-    big = pltpu.VMEM((8, 8, ROWS, LN), F32)
+    big = pltpu.VMEM((8, 2, 4, ROWS, LN), F32)
     return pl.pallas_call(
         kernel,
         out_shape=jax.ShapeDtypeStruct((2, PL3, NG, NG), F32),
-        in_specs=[smem, smem] + [pl.BlockSpec(memory_space=pl.ANY)] * 6,
+        in_specs=[smem, smem] + [pl.BlockSpec(memory_space=pl.ANY)] * 5,
         out_specs=vmem,
         scratch_shapes=[
             big, big, big, big, big, big,
@@ -303,8 +352,12 @@
             pltpu.VMEM((3, 3, NG, LN), F32),
             pltpu.VMEM(bands.shape, F32),
             pltpu.VMEM(occupied.shape, F32),
-            *(pltpu.VMEM(m.shape, BF16) for m in constants),
-            pltpu.SemaphoreType.DMA((6,)),
+            pltpu.VMEM((2, NG, NG), BF16),
+            pltpu.VMEM((2, 2, 256, 256), BF16),
+            pltpu.VMEM((2, NG, NG), BF16),
+            pltpu.VMEM((2, NG, NG), BF16),
+            pltpu.VMEM((2, NG, NG), BF16),
+            pltpu.SemaphoreType.DMA((5,)),
             pltpu.SemaphoreType.DMA((12,)),
             pltpu.SemaphoreType.DMA((12,)),
             pltpu.SemaphoreType.DMA((18,)),

time: 119 us -> 116 us (0.975); the launches traced: 119 us -> 114 us
  Pallas kernels: 116 us -> 112 us
    pallas_call x1, Pallas kernels: 116 us -> 112 us  [shards(): pl.pallas_call(kernel, out_shape=jax.ShapeDtypeStruct((2, PL3, NG, NG), F...]
where the time goes in v5:
time: 116 us; the launch traced here: 114 us
  Pallas kernels  112 us (97%)
  local copies, waits for them, and re-layouts  2.42 us (2%)
    pallas_call x1, Pallas kernels, shards(): pl.pallas_call(kernel, out_shape=jax.ShapeDtypeStruct((2, PL3, NG, NG), F...  112 us
    unnamed x1, local copies, waits for them, and re-layouts  2.42 us

profile of v5, /device:TPU:8, one launch (start us, length us, event | category | flops | bytes accessed | tf_op | source)
XLA Modules:
  0.0 114.0 jit_solution(16293735936624293733)
XLA Ops:
  0.0 111.6 %shard_map.73 = f32[2,3,192,192]{3,2,1,0:T(8,128)} custom-call(s32[2]{0:T(128)} %occ_index.1, s32[2]{0:T(128)} %band_pick.1, f32[2,3,192,192]{3,2,1,0:T(8,128)} %bands_in.1, f32[4,3,192,192]{3,2,1,0:T(8,128)} %occupied_in.1, bf16[4,2,192,192]{3,2,1,0:T(8,128)(2,1)} %constant.6.clone.rows_in, bf16[2,2,256,256]{3,2,1,0:T(8,128)(2,1)} %constant.7.clone.zmat_in, ...), custom_call_target="tpu_custom_call" | custom-call | tf_op jit(solution)/shard_map/pallas_call | solution.py:337
  111.6 2.4 %copy.9 = f32[2,3,192,192]{3,2,1,0:T(8,128)} copy(f32[2,3,192,192]{3,2,1,0:T(8,128)} %shard_map.73) | data formatting | bytes 1769472

commit v6 on v5

--- a/solution.py
+++ b/solution.py
@@ -187,49 +187,44 @@
 
     near = pl.ds(0, 3)
 
-    def forth_z(chunk, rows):
+    def z_then(src, dst, k, rows):
         for z in z_peers:
-            push(send1.at[z, :, near, rows], mid1.at[zz, :, near, rows], chunk, at(z, yh, xx))
-            push(send1.at[z, 0, 3, rows], mid1.at[zz, 0, 3, rows], chunk, at(z, yh, up))
-            push(send1.at[z, 1, 3, rows], mid1.at[zz, 1, 3, rows], chunk, at(z, yh, down))
-        push(send1.at[zz, 0, 3, rows], mid1.at[zz, 0, 3, rows], chunk, at(zz, yh, up))
-        push(send1.at[zz, 1, 3, rows], mid1.at[zz, 1, 3, rows], chunk, at(zz, yh, down))
-        pltpu.make_async_copy(
-            send1.at[zz, :, near, rows], mid1.at[zz, :, near, rows], r_sem.at[chunk]
-        ).start()
-
-    def forth_xy(chunk):
-        rows, k = pl.ds(*CHUNKS[chunk]), 3 + chunk
+            push(src.at[z, :, near, rows], dst.at[zz, :, near, rows], k, at(z, yh, xx))
+            push(src.at[z, 0, 3, rows], dst.at[zz, 0, 3, rows], k, at(z, yh, up))
+            push(src.at[z, 1, 3, rows], dst.at[zz, 1, 3, rows], k, at(z, yh, down))
+        push(src.at[zz, 0, 3, rows], dst.at[zz, 0, 3, rows], k, at(zz, yh, up))
+        push(src.at[zz, 1, 3, rows], dst.at[zz, 1, 3, rows], k, at(zz, yh, down))
+        pltpu.make_async_copy(src.at[zz, :, near, rows], dst.at[zz, :, near, rows], r_sem.at[k]).start()
+
+    def plane(src, dst, k, rows):
         for r, x in ((0, down), (2, up), (1, xx)):
             for y in range(2):
-                push(mid1.at[:, y, r, rows], recv1.at[:, yh, 2 - r, rows], k, at(zz, y, x, **across))
-        push(mid1.at[:, 0, 3, rows], recv1.at[:, yh, 3, rows], k, at(zz, 0, up, **across))
-        push(mid1.at[:, 1, 3, rows], recv1.at[:, yh, 3, rows], k, at(zz, 1, down, **across))
-
-    def back_xy(chunk):
-        rows, k = pl.ds(*CHUNKS[chunk]), 6 + chunk
-        for r, x in ((0, down), (2, up), (1, xx)):
-            for y in range(2):
-                push(send2.at[:, y, r, rows], mid2.at[:, yh, 2 - r, rows], k, at(zz, y, x, **across))
-        push(send2.at[:, 0, 3, rows], mid2.at[:, yh, 3, rows], k, at(zz, 0, up, **across))
-        push(send2.at[:, 1, 3, rows], mid2.at[:, yh, 3, rows], k, at(zz, 1, down, **across))
-
-    def back_z(chunk):
-        rows, k = pl.ds(*CHUNKS[chunk]), 9 + chunk
+                push(src.at[:, y, r, rows], dst.at[:, yh, 2 - r, rows], k, at(zz, y, x, **across))
+        push(src.at[:, 0, 3, rows], dst.at[:, yh, 3, rows], k, at(zz, 0, up, **across))
+        push(src.at[:, 1, 3, rows], dst.at[:, yh, 3, rows], k, at(zz, 1, down, **across))
+
+    def then_z(src, dst, k, rows):
         for z in z_peers:
-            push(mid2.at[z, :, near, rows], recv2.at[zz, :, near, rows], k, at(z, yh, xx))
-            push(mid2.at[z, :, 3, rows], recv2.at[zz, :, 3, rows], k, at(z, yh, turn))
-        push(mid2.at[zz, :, 3, rows], recv2.at[zz, :, 3, rows], k, at(zz, yh, turn))
-        pltpu.make_async_copy(mid2.at[zz, :, near, rows], recv2.at[zz, :, near, rows], r_sem.at[k]).start()
-
-    def arrived(phase, chunk):
-        ref = (mid1, recv1, mid2, recv2)[phase].at[:, :, :, pl.ds(*CHUNKS[chunk])]
-        pltpu.make_async_copy(ref, ref, r_sem.at[phase * 3 + chunk]).wait()
-
-    def sent(phase, chunk):
-        ref = (send1, mid1, send2, mid2)[phase].reshape(SL, ROWS, LN)
-        ref = ref.at[pl.ds(0, WIDE if phase % 3 == 0 else SL), pl.ds(*CHUNKS[chunk])]
-        pltpu.make_async_copy(ref, ref, s_sem.at[phase * 3 + chunk]).wait()
+            push(src.at[z, :, near, rows], dst.at[zz, :, near, rows], k, at(z, yh, xx))
+            push(src.at[z, :, 3, rows], dst.at[zz, :, 3, rows], k, at(z, yh, turn))
+        push(src.at[zz, :, 3, rows], dst.at[zz, :, 3, rows], k, at(zz, yh, turn))
+        pltpu.make_async_copy(src.at[zz, :, near, rows], dst.at[zz, :, near, rows], r_sem.at[k]).start()
+
+    stages = ((send1, mid1), (mid1, recv1), (send2, mid2), (mid2, recv2))
+
+    def go(chunk, stage):
+        along = (z_then, plane, plane, then_z) if chunk == 0 else (plane, then_z, z_then, plane)
+        along[stage](*stages[stage], stage * 3 + chunk, pl.ds(*CHUNKS[chunk]))
+
+    def arrived(chunk, stage, k=None, rows=None):
+        ref = stages[stage][1].at[:, :, :, rows or pl.ds(*CHUNKS[chunk])]
+        pltpu.make_async_copy(ref, ref, r_sem.at[k or stage * 3 + chunk]).wait()
+
+    def sent(chunk, stage, k=None, rows=None):
+        ref = stages[stage][0].reshape(SL, ROWS, LN)
+        wide = WIDE if (stage % 3 == 0) == (chunk == 0) else SL
+        ref = ref.at[pl.ds(0, wide), rows or pl.ds(*CHUNKS[chunk])]
+        pltpu.make_async_copy(ref, ref, s_sem.at[k or stage * 3 + chunk]).wait()
 
     low_lane = lax.broadcasted_iota(jnp.int32, (96, LN), 1) < 64
 
@@ -275,7 +270,7 @@
         blocks = along_z(*blocks, zmat)
         o0, o1 = orb[w, x, 0], orb[w, x, 1]
         for b, o in enumerate((o0, o0, o1)):
-            acc[x, b] = -blocks[b] * o if w == 0 else acc[x, b] - blocks[b] * o
+            acc[x, b] = -blocks[b] * o if w == 1 else acc[x, b] - blocks[b] * o
 
     join(0)
     for k in range(6):
@@ -283,39 +278,41 @@
             join(k + 1)
         forward(k)
         if k < 3:
-            forth_z(0, pl.ds(8 * k, 8))
+            z_then(send1, mid1, 0, pl.ds(8 * k, 8))
 
     def conv(chunk):
-        arrived(1, chunk)
+        arrived(chunk, 1)
         middle(chunk)
-        back_xy(chunk)
-
+        go(chunk, 2)
+
+    go(1, 0)
+    sent(1, 0)
+    go(2, 0)
+    arrived(1, 0)
     sent(0, 0)
-    forth_z(1, pl.ds(*CHUNKS[1]))
+    go(1, 1)
     arrived(0, 0)
-    forth_xy(0)
+    go(0, 1)
+    arrived(2, 0)
+    sent(1, 1)
+    go(2, 1)
     conv(0)
-    sent(0, 1)
-    forth_z(2, pl.ds(*CHUNKS[2]))
-    arrived(2, 0)
-    back_z(0)
-    arrived(0, 1)
-    forth_xy(1)
-    arrived(0, 2)
-    forth_xy(2)
     conv(1)
     conv(2)
-    arrived(2, 1)
-    back_z(1)
+    arrived(1, 2)
+    go(1, 3)
+    arrived(0, 2)
+    for x in range(3):
+        then_z(mid2, recv2, 11 + x if x else 9, pl.ds(8 * x, 8))
     arrived(2, 2)
-    back_z(2)
-    arrived(3, 0)
-    arrived(3, 1)
-    for x in range(3):
+    go(2, 3)
+    arrived(1, 3)
+    arrived(2, 3)
+    for x in range(3):
+        finish(1, x)
+    for x in range(3):
+        arrived(0, 3, 11 + x if x else 9, pl.ds(8 * x, 8))
         finish(0, x)
-    arrived(3, 2)
-    for x in range(3):
-        finish(1, x)
         for p in range(2):
             out[p, x] = jnp.concatenate([acc[x, p], acc[x, 2][:, p * 64 : (p + 1) * 64]], 1)
 
@@ -323,10 +320,10 @@
         first[k].wait_send()
         second[k].wait_send()
         third[k].wait_send()
-    sent(0, 2)
-    for phase in range(1, 4):
-        for chunk in range(3):
-            sent(phase, chunk)
+    for chunk, stage in ((2, 0), (0, 1), (2, 1), (0, 2), (1, 2), (2, 2), (1, 3), (2, 3)):
+        sent(chunk, stage)
+    for x in range(3):
+        sent(0, 3, 11 + x if x else 9, pl.ds(8 * x, 8))
 
 
 def shards(bands, occupied, occ_index, band_pick):
@@ -358,8 +355,8 @@
             pltpu.VMEM((2, NG, NG), BF16),
             pltpu.VMEM((2, NG, NG), BF16),
             pltpu.SemaphoreType.DMA((5,)),
-            pltpu.SemaphoreType.DMA((12,)),
-            pltpu.SemaphoreType.DMA((12,)),
+            pltpu.SemaphoreType.DMA((14,)),
+            pltpu.SemaphoreType.DMA((14,)),
             pltpu.SemaphoreType.DMA((18,)),
             pltpu.SemaphoreType.DMA((18,)),
         ],

time: 116 us -> 106 us (0.914)
  Pallas kernels: 112 us -> 103 us
    pallas_call x1, Pallas kernels: 112 us -> 103 us  [shards(): pl.pallas_call(kernel, out_shape=jax.ShapeDtypeStruct((2, PL3, NG, NG), F...]
where the time goes in v6:
time: 106 us; the launch traced here: 105 us
  Pallas kernels  103 us (97%)
  local copies, waits for them, and re-layouts  2.42 us (2%)
    pallas_call x1, Pallas kernels, shards(): pl.pallas_call(kernel, out_shape=jax.ShapeDtypeStruct((2, PL3, NG, NG), F...  103 us
    unnamed x1, local copies, waits for them, and re-layouts  2.42 us

profile of v6, /device:TPU:8, one launch (start us, length us, event | category | flops | bytes accessed | tf_op | source)
XLA Modules:
  0.0 105.0 jit_solution(313230750990458358)
XLA Ops:
  0.0 102.6 %shard_map.73 = f32[2,3,192,192]{3,2,1,0:T(8,128)} custom-call(s32[2]{0:T(128)} %occ_index.1, s32[2]{0:T(128)} %band_pick.1, f32[2,3,192,192]{3,2,1,0:T(8,128)} %bands_in.1, f32[4,3,192,192]{3,2,1,0:T(8,128)} %occupied_in.1, bf16[4,2,192,192]{3,2,1,0:T(8,128)(2,1)} %constant.6.clone.rows_in, bf16[2,2,256,256]{3,2,1,0:T(8,128)(2,1)} %constant.7.clone.zmat_in, ...), custom_call_target="tpu_custom_call" | custom-call | tf_op jit(solution)/shard_map/pallas_call | solution.py:334
  102.6 2.4 %copy.9 = f32[2,3,192,192]{3,2,1,0:T(8,128)} copy(f32[2,3,192,192]{3,2,1,0:T(8,128)} %shard_map.73) | data formatting | bytes 1769472

commit v7 on v6

--- a/solution.py
+++ b/solution.py
@@ -15,7 +15,7 @@
 omega = 0.106
 NG, SL, PL3, LN = 192, 64, 3, 128
 ROWS = 56
-CHUNKS = ((0, 24), (24, 16), (40, 16))
+CHUNKS = ((0, 24), (24, 15), (40, 15))
 BLOCKS = (range(0, 8), range(8, 13), range(13, 18))
 WIDE = 58
 Z_STEPS = (1, 7, 2, 6, 3, 5, 4)
@@ -92,15 +92,17 @@
 def kernel(
     occ_index, band_pick, bands_in, occupied_in, rows_in, zmat_in, xmat_in, out,
     send1, mid1, recv1, send2, mid2, recv2, own, got, part, cross, full, target, orb, table, acc,
-    bands, occupied, cas, zmat, xmat, cas_t, xmat_t,
+    bands, occupied0, occupied1, occupied2, cas, zmat, xmat, cas_t, xmat_t,
     load, s_sem, r_sem, xs, xr,
 ):
     band, slab = lax.axis_index("band"), lax.axis_index("slab")
     y_lo, core = band // 2, band % 2
     zz, xy = slab // 8, slab % 8
     yh, xx = xy // 4, xy % 4
+    occupied = (occupied0, occupied1, occupied2)
     pairs = (
-        (occupied_in, occupied), (bands_in, bands), (rows_in.at[xx], cas), (zmat_in, zmat), (xmat_in.at[xx], xmat)
+        *((occupied_in.at[:, x], occupied[x]) for x in range(3)),
+        (bands_in, bands), (rows_in.at[xx], cas), (zmat_in, zmat), (xmat_in.at[xx], xmat)
     )
     loads = [pltpu.make_async_copy(src, dst, load.at[k]) for k, (src, dst) in enumerate(pairs)]
     for copy in loads:
@@ -122,15 +124,14 @@
     for where in greeted:
         pl.semaphore_signal(barrier, inc=1, device_id=where, device_id_type=MESH)
 
-    def pack(w):
+    def pack(w, x):
         which = occ_index[w]
         mine = which // 4 == band
-        for x in range(3):
-            v = occupied[which % 4, x]
-            v = jnp.where(mine, v, jnp.zeros_like(v))
-            own[w, x, :NG] = v[:, :LN]
-            high = v[:, LN:]
-            own[w, x, NG:] = jnp.concatenate([high[:96], high[96:]], 1)
+        v = occupied[x][which % 4]
+        v = jnp.where(mine, v, jnp.zeros_like(v))
+        own[w, x, :NG] = v[:, :LN]
+        high = v[:, LN:]
+        own[w, x, NG:] = jnp.concatenate([high[:96], high[96:]], 1)
 
     def hop(src, dst, k, where):
         return pltpu.make_async_remote_copy(
@@ -146,25 +147,27 @@
     third = [hop(full.at[w, x, mine_rows], full.at[w, x, mine_rows], 12 + w * 3 + x, partner) for w, x in units]
 
     loads[0].wait()
-    pack(0)
+    pack(0, 0)
     pl.semaphore_wait(barrier, len(greeted))
-    for k in range(3):
-        first[k].start()
-    pack(1)
-    for k in range(3, 6):
+    first[0].start()
+    for k in range(1, 6):
+        w, x = units[k]
+        if w == 0:
+            loads[x].wait()
+        pack(w, x)
         first[k].start()
     for k, (w, x) in enumerate(units):
         first[k].wait_recv()
         part[w, x] = own[w, x, mine_rows] + got[w, x]
         second[k].start()
 
-    loads[1].wait()
+    loads[3].wait()
     for x in range(3):
         t0, t1 = bands[band_pick[0], x], bands[band_pick[1], x]
         target[x, 0] = t0[:, :LN]
         target[x, 1] = t1[:, :LN]
         target[x, 2] = jnp.concatenate([t0[:, LN:], t1[:, LN:]], 1)
-    for copy in loads[2:]:
+    for copy in loads[4:]:
         copy.wait()
     for h in range(2):
         cas_t[h] = cas[h].astype(F32).T.astype(BF16)
@@ -274,11 +277,11 @@
 
     join(0)
     for k in range(6):
-        if k < 5:
-            join(k + 1)
         forward(k)
         if k < 3:
             z_then(send1, mid1, 0, pl.ds(8 * k, 8))
+        for j in ((1, 2), (3,), (4,), (5,), (), ())[k]:
+            join(j)
 
     def conv(chunk):
         arrived(chunk, 1)
@@ -348,22 +351,22 @@
             pltpu.VMEM((3, 2, NG, LN), F32),
             pltpu.VMEM((3, 3, NG, LN), F32),
             pltpu.VMEM(bands.shape, F32),
-            pltpu.VMEM(occupied.shape, F32),
+            *([pltpu.VMEM((occupied.shape[0], NG, NG), F32)] * 3),
             pltpu.VMEM((2, NG, NG), BF16),
             pltpu.VMEM((2, 2, 256, 256), BF16),
             pltpu.VMEM((2, NG, NG), BF16),
             pltpu.VMEM((2, NG, NG), BF16),
             pltpu.VMEM((2, NG, NG), BF16),
-            pltpu.SemaphoreType.DMA((5,)),
+            pltpu.SemaphoreType.DMA((7,)),
             pltpu.SemaphoreType.DMA((14,)),
             pltpu.SemaphoreType.DMA((14,)),
             pltpu.SemaphoreType.DMA((18,)),
             pltpu.SemaphoreType.DMA((18,)),
         ],
         compiler_params=pltpu.CompilerParams(
-            collective_id=0, has_side_effects=True, vmem_limit_bytes=62 * 1024 * 1024
+            collective_id=0, has_side_effects=True, vmem_limit_bytes=40 * 1024 * 1024
         ),
-    )(occ_index, band_pick, bands, occupied, *constants)
+    )(*(pltpu.with_memory_space_constraint(a, pltpu.HBM) for a in (occ_index, band_pick, bands, occupied, *constants)))
 
 
 def solution(mesh):

time: 106 us -> 99.8 us (0.942)
  Pallas kernels: 103 us -> 97.3 us
  local copies, waits for them, and re-layouts: 2.42 us -> 1.02 us
    pallas_call x1, Pallas kernels: 103 us -> 97.3 us  [shards(): pl.pallas_call(kernel, out_shape=jax.ShapeDtypeStruct((2, PL3, NG, NG), F...]
    unnamed x1, local copies, waits for them, and re-layouts: 2.42 us -> 1.02 us
where the time goes in v7:
time: 99.8 us; the launch traced here: 98.4 us
  Pallas kernels  97.3 us (97%)
  local copies, waits for them, and re-layouts  1.02 us (1%)
    pallas_call x1, Pallas kernels, shards(): pl.pallas_call(kernel, out_shape=jax.ShapeDtypeStruct((2, PL3, NG, NG), F...  97.3 us

profile of v7, /device:TPU:8, one launch (start us, length us, event | category | flops | bytes accessed | tf_op | source)
XLA Modules:
  0.0 98.4 jit_solution(13753313402703432168)
XLA Ops:
  0.0 97.3 %shard_map.73 = f32[2,3,192,192]{3,2,1,0:T(8,128)S(1)} custom-call(s32[2]{0:T(128)} %occ_index.1, s32[2]{0:T(128)} %band_pick.1, f32[2,3,192,192]{3,2,1,0:T(8,128)} %bands_in.1, f32[4,3,192,192]{3,2,1,0:T(8,128)} %occupied_in.1, bf16[4,2,192,192]{3,2,1,0:T(8,128)(2,1)} %constant.6.clone.rows_in, bf16[2,2,256,256]{3,2,1,0:T(8,128)(2,1)} %constant.7.clone.zmat_in, ...), custom_call_target="tpu_custom_call" | custom-call | tf_op jit(solution)/shard_map/pallas_call | solution.py:337
  97.3 1.0 %copy.9 = f32[2,3,192,192]{3,2,1,0:T(8,128)} copy(f32[2,3,192,192]{3,2,1,0:T(8,128)S(1)} %shard_map.73) | data formatting | bytes 1769472

commit v8 on v7

--- a/solution.py
+++ b/solution.py
@@ -18,7 +18,7 @@
 CHUNKS = ((0, 24), (24, 15), (40, 15))
 BLOCKS = (range(0, 8), range(8, 13), range(13, 18))
 WIDE = 58
-Z_STEPS = (1, 7, 2, 6, 3, 5, 4)
+Z_STEPS = (1, 7, 2, 6, 3, 5)
 
 
 def row_of(n, x):
@@ -48,7 +48,7 @@
     for x in range(4):
         device = slot // 4 * 4 + (x + slot % 4 - 1) % 4
         rows.append(split_host(cas[(np.arange(3)[:, None] * SL + device[None, :]).reshape(-1)]))
-        across.append(split_host(cas[:, (3 * device[None, :] + np.arange(PL3)[:, None]).reshape(-1)]))
+        across.append(split_host(cas[(3 * device[None, :] + np.arange(PL3)[:, None]).reshape(-1)]))
     return [np.stack(rows), split_host(np.stack([first, second])), np.stack(across)]
 
 
@@ -92,7 +92,7 @@
 def kernel(
     occ_index, band_pick, bands_in, occupied_in, rows_in, zmat_in, xmat_in, out,
     send1, mid1, recv1, send2, mid2, recv2, own, got, part, cross, full, target, orb, table, acc,
-    bands, occupied0, occupied1, occupied2, cas, zmat, xmat, cas_t, xmat_t,
+    bands, occupied0, occupied1, occupied2, raw, zmat, raw_x, cas, xmat, cas_t, xmat_t, work, turned_work,
     load, s_sem, r_sem, xs, xr,
 ):
     band, slab = lax.axis_index("band"), lax.axis_index("slab")
@@ -102,13 +102,15 @@
     occupied = (occupied0, occupied1, occupied2)
     pairs = (
         *((occupied_in.at[:, x], occupied[x]) for x in range(3)),
-        (bands_in, bands), (rows_in.at[xx], cas), (zmat_in, zmat), (xmat_in.at[xx], xmat)
+        (bands_in, bands), (rows_in.at[xx], raw), (zmat_in, zmat), (xmat_in.at[xx], raw_x)
     )
     loads = [pltpu.make_async_copy(src, dst, load.at[k]) for k, (src, dst) in enumerate(pairs)]
     for copy in loads:
         copy.start()
 
-    z_peers = [(zz + d) % 8 for d in Z_STEPS]
+    z_peers = [(d, (zz + d) % 8) for d in Z_STEPS]
+    z_up, z_down, z_up3, z_down3 = ((zz + d) % 8 for d in (1, 7, 3, 5))
+    z_turn = (zz + 1 + 6 * yh) % 8
     up, down = (xx + 1) % 4, (xx + 3) % 4
     turn = (xx + 1 + 2 * yh) % 4
     partner = {"band": y_lo * 2 + (1 - core)}
@@ -117,9 +119,9 @@
     def at(z, y, x, **more):
         return {"slab": z * 8 + y * 4 + x, **more}
 
-    greeted = [partner] + [at(z, yh, xx) for z in z_peers]
-    greeted += [at(z, yh, x) for z in [zz] + z_peers for x in (up, down)]
-    greeted += [at(zz, y, x, **across) for y in (0, 1) for x in (down, xx, up)]
+    greeted = [partner] + [at(z, yh, x) for _, z in z_peers for x in (xx, up, down)]
+    greeted += [at(zz, yh, x) for x in (up, down)]
+    greeted += [at(z, y, x, **across) for z in (zz, z_up, z_down) for y in (0, 1) for x in (down, xx, up)]
     barrier = pltpu.get_barrier_semaphore()
     for where in greeted:
         pl.semaphore_signal(barrier, inc=1, device_id=where, device_id_type=MESH)
@@ -169,9 +171,15 @@
         target[x, 2] = jnp.concatenate([t0[:, LN:], t1[:, LN:]], 1)
     for copy in loads[4:]:
         copy.wait()
-    for h in range(2):
-        cas_t[h] = cas[h].astype(F32).T.astype(BF16)
-        xmat_t[h] = xmat[h].astype(F32).T.astype(BF16)
+    for source, rows, columns in ((raw, cas, cas_t), (raw_x, xmat_t, xmat)):
+        for h in range(2):
+            work[...] = source[h].astype(F32)
+            for z in range(8):
+                for j in range(3):
+                    rolled = pl.multiple_of(j * SL + ((zz + z) % 8) * 8, 8)
+                    turned_work[pl.ds(j * SL + z * 8, 8), :] = work[pl.ds(rolled, 8), :]
+            rows[h] = turned_work[...].astype(BF16)
+            columns[h] = turned_work[...].T.astype(BF16)
 
     for j in range(3):
         ky = signed_square(jnp.full((NG, LN), j * SL, jnp.int32) + slab)
@@ -191,32 +199,40 @@
     near = pl.ds(0, 3)
 
     def z_then(src, dst, k, rows):
-        for z in z_peers:
-            push(src.at[z, :, near, rows], dst.at[zz, :, near, rows], k, at(z, yh, xx))
-            push(src.at[z, 0, 3, rows], dst.at[zz, 0, 3, rows], k, at(z, yh, up))
-            push(src.at[z, 1, 3, rows], dst.at[zz, 1, 3, rows], k, at(z, yh, down))
-        push(src.at[zz, 0, 3, rows], dst.at[zz, 0, 3, rows], k, at(zz, yh, up))
-        push(src.at[zz, 1, 3, rows], dst.at[zz, 1, 3, rows], k, at(zz, yh, down))
-        pltpu.make_async_copy(src.at[zz, :, near, rows], dst.at[zz, :, near, rows], r_sem.at[k]).start()
-
-    def plane(src, dst, k, rows):
-        for r, x in ((0, down), (2, up), (1, xx)):
-            for y in range(2):
-                push(src.at[:, y, r, rows], dst.at[:, yh, 2 - r, rows], k, at(zz, y, x, **across))
-        push(src.at[:, 0, 3, rows], dst.at[:, yh, 3, rows], k, at(zz, 0, up, **across))
-        push(src.at[:, 1, 3, rows], dst.at[:, yh, 3, rows], k, at(zz, 1, down, **across))
+        for d, z in z_peers:
+            push(src.at[d, :, near, rows], dst.at[8 - d, :, near, rows], k, at(z, yh, xx))
+            push(src.at[d, 0, 3, rows], dst.at[8 - d, 0, 3, rows], k, at(z, yh, up))
+            push(src.at[d, 1, 3, rows], dst.at[8 - d, 1, 3, rows], k, at(z, yh, down))
+        for y, z, x in ((0, z_up3, up), (1, z_down3, down)):
+            push(src.at[4, y, near, rows], dst.at[4, y, near, rows], k, at(z, yh, xx))
+            push(src.at[4, y, 3, rows], dst.at[4, y, 3, rows], k, at(z, yh, x))
+        push(src.at[0, 0, 3, rows], dst.at[0, 0, 3, rows], k, at(zz, yh, up))
+        push(src.at[0, 1, 3, rows], dst.at[0, 1, 3, rows], k, at(zz, yh, down))
+        pltpu.make_async_copy(src.at[0, :, near, rows], dst.at[0, :, near, rows], r_sem.at[k]).start()
+
+    def plane(src, dst, k, rows, ahead):
+        hops = [(y, r, 2 - r, x) for r, x in ((0, down), (2, up), (1, xx)) for y in range(2)]
+        for y, r, q, x in hops + [(0, 3, 3, up), (1, 3, 3, down)]:
+            z = z_turn if ahead else (z_up, z_down)[y]
+            push(src.at[4, y, r, rows], dst.at[4, yh, q, rows], k, at(z, y, x, **across))
+            for part in (pl.ds(0, 4), pl.ds(5, 3)):
+                push(src.at[part, y, r, rows], dst.at[part, yh, q, rows], k, at(zz, y, x, **across))
 
     def then_z(src, dst, k, rows):
-        for z in z_peers:
-            push(src.at[z, :, near, rows], dst.at[zz, :, near, rows], k, at(z, yh, xx))
-            push(src.at[z, :, 3, rows], dst.at[zz, :, 3, rows], k, at(z, yh, turn))
-        push(src.at[zz, :, 3, rows], dst.at[zz, :, 3, rows], k, at(zz, yh, turn))
-        pltpu.make_async_copy(src.at[zz, :, near, rows], dst.at[zz, :, near, rows], r_sem.at[k]).start()
-
+        for d, z in z_peers:
+            push(src.at[d, :, near, rows], dst.at[8 - d, :, near, rows], k, at(z, yh, xx))
+            push(src.at[d, :, 3, rows], dst.at[8 - d, :, 3, rows], k, at(z, yh, turn))
+        for y, z in ((0, z_up3), (1, z_down3)):
+            push(src.at[4, y, near, rows], dst.at[4, y, near, rows], k, at(z, yh, xx))
+            push(src.at[4, y, 3, rows], dst.at[4, y, 3, rows], k, at(z, yh, turn))
+        push(src.at[0, :, 3, rows], dst.at[0, :, 3, rows], k, at(zz, yh, turn))
+        pltpu.make_async_copy(src.at[0, :, near, rows], dst.at[0, :, near, rows], r_sem.at[k]).start()
+
+    plane_first, plane_last = functools.partial(plane, ahead=True), functools.partial(plane, ahead=False)
     stages = ((send1, mid1), (mid1, recv1), (send2, mid2), (mid2, recv2))
 
     def go(chunk, stage):
-        along = (z_then, plane, plane, then_z) if chunk == 0 else (plane, then_z, z_then, plane)
+        along = (z_then, plane_last, plane_first, then_z) if chunk == 0 else (plane_first, then_z, z_then, plane_last)
         along[stage](*stages[stage], stage * 3 + chunk, pl.ds(*CHUNKS[chunk]))
 
     def arrived(chunk, stage, k=None, rows=None):
@@ -355,8 +371,8 @@
             pltpu.VMEM((2, NG, NG), BF16),
             pltpu.VMEM((2, 2, 256, 256), BF16),
             pltpu.VMEM((2, NG, NG), BF16),
-            pltpu.VMEM((2, NG, NG), BF16),
-            pltpu.VMEM((2, NG, NG), BF16),
+            *([pltpu.VMEM((2, NG, NG), BF16)] * 4),
+            *([pltpu.VMEM((NG, NG), F32)] * 2),
             pltpu.SemaphoreType.DMA((7,)),
             pltpu.SemaphoreType.DMA((14,)),
             pltpu.SemaphoreType.DMA((14,)),

time: 99.8 us -> 107 us (1.072)
  Pallas kernels: 97.3 us -> 105 us
    pallas_call x1, Pallas kernels: 97.3 us -> 105 us  [shards(): pl.pallas_call(kernel, out_shape=jax.ShapeDtypeStruct((2, PL3, NG, NG), F...]
where the time goes in v8:
time: 107 us; the launch traced here: 106 us
  Pallas kernels  105 us (98%)
    pallas_call x1, Pallas kernels, shards(): pl.pallas_call(kernel, out_shape=jax.ShapeDtypeStruct((2, PL3, NG, NG), F...  105 us

profile of v8, /device:TPU:8, one launch (start us, length us, event | category | flops | bytes accessed | tf_op | source)
XLA Modules:
  0.0 105.6 jit_solution(4979675775694321024)
XLA Ops:
  0.0 104.6 %shard_map.73 = f32[2,3,192,192]{3,2,1,0:T(8,128)S(1)} custom-call(s32[2]{0:T(128)} %occ_index.1, s32[2]{0:T(128)} %band_pick.1, f32[2,3,192,192]{3,2,1,0:T(8,128)} %bands_in.1, f32[4,3,192,192]{3,2,1,0:T(8,128)} %occupied_in.1, bf16[4,2,192,192]{3,2,1,0:T(8,128)(2,1)} %constant.6.clone.rows_in, bf16[2,2,256,256]{3,2,1,0:T(8,128)(2,1)} %constant.7.clone.zmat_in, ...), custom_call_target="tpu_custom_call" | custom-call | tf_op jit(solution)/shard_map/pallas_call | solution.py:353
  104.6 1.0 copy.9

commit v9 on v7

--- a/solution.py
+++ b/solution.py
@@ -17,7 +17,7 @@
 ROWS = 56
 CHUNKS = ((0, 24), (24, 15), (40, 15))
 BLOCKS = (range(0, 8), range(8, 13), range(13, 18))
-WIDE = 58
+WIDE = 56
 Z_STEPS = (1, 7, 2, 6, 3, 5, 4)
 
 
@@ -109,8 +109,7 @@
         copy.start()
 
     z_peers = [(zz + d) % 8 for d in Z_STEPS]
-    up, down = (xx + 1) % 4, (xx + 3) % 4
-    turn = (xx + 1 + 2 * yh) % 4
+    up, over, down = (xx + 1) % 4, (xx + 2) % 4, (xx + 3) % 4
     partner = {"band": y_lo * 2 + (1 - core)}
     across = {"band": (1 - y_lo) * 2 + core}
 
@@ -118,8 +117,7 @@
         return {"slab": z * 8 + y * 4 + x, **more}
 
     greeted = [partner] + [at(z, yh, xx) for z in z_peers]
-    greeted += [at(z, yh, x) for z in [zz] + z_peers for x in (up, down)]
-    greeted += [at(zz, y, x, **across) for y in (0, 1) for x in (down, xx, up)]
+    greeted += [at(zz, y, x, **across) for y in (0, 1) for x in (down, xx, up, over)]
     barrier = pltpu.get_barrier_semaphore()
     for where in greeted:
         pl.semaphore_signal(barrier, inc=1, device_id=where, device_id_type=MESH)
@@ -188,35 +186,20 @@
             src_ref=src, dst_ref=dst, send_sem=s_sem.at[k], recv_sem=r_sem.at[k], device_id=where, device_id_type=MESH
         ).start()
 
-    near = pl.ds(0, 3)
-
-    def z_then(src, dst, k, rows):
+    def along_zz(src, dst, k, rows):
         for z in z_peers:
-            push(src.at[z, :, near, rows], dst.at[zz, :, near, rows], k, at(z, yh, xx))
-            push(src.at[z, 0, 3, rows], dst.at[zz, 0, 3, rows], k, at(z, yh, up))
-            push(src.at[z, 1, 3, rows], dst.at[zz, 1, 3, rows], k, at(z, yh, down))
-        push(src.at[zz, 0, 3, rows], dst.at[zz, 0, 3, rows], k, at(zz, yh, up))
-        push(src.at[zz, 1, 3, rows], dst.at[zz, 1, 3, rows], k, at(zz, yh, down))
-        pltpu.make_async_copy(src.at[zz, :, near, rows], dst.at[zz, :, near, rows], r_sem.at[k]).start()
+            push(src.at[z, :, :, rows], dst.at[zz, :, :, rows], k, at(z, yh, xx))
+        pltpu.make_async_copy(src.at[zz, :, :, rows], dst.at[zz, :, :, rows], r_sem.at[k]).start()
 
     def plane(src, dst, k, rows):
-        for r, x in ((0, down), (2, up), (1, xx)):
+        for r, q, x in ((0, 2, down), (2, 0, up), (3, 3, over), (1, 1, xx)):
             for y in range(2):
-                push(src.at[:, y, r, rows], dst.at[:, yh, 2 - r, rows], k, at(zz, y, x, **across))
-        push(src.at[:, 0, 3, rows], dst.at[:, yh, 3, rows], k, at(zz, 0, up, **across))
-        push(src.at[:, 1, 3, rows], dst.at[:, yh, 3, rows], k, at(zz, 1, down, **across))
-
-    def then_z(src, dst, k, rows):
-        for z in z_peers:
-            push(src.at[z, :, near, rows], dst.at[zz, :, near, rows], k, at(z, yh, xx))
-            push(src.at[z, :, 3, rows], dst.at[zz, :, 3, rows], k, at(z, yh, turn))
-        push(src.at[zz, :, 3, rows], dst.at[zz, :, 3, rows], k, at(zz, yh, turn))
-        pltpu.make_async_copy(src.at[zz, :, near, rows], dst.at[zz, :, near, rows], r_sem.at[k]).start()
+                push(src.at[:, y, r, rows], dst.at[:, yh, q, rows], k, at(zz, y, x, **across))
 
     stages = ((send1, mid1), (mid1, recv1), (send2, mid2), (mid2, recv2))
 
     def go(chunk, stage):
-        along = (z_then, plane, plane, then_z) if chunk == 0 else (plane, then_z, z_then, plane)
+        along = (along_zz, plane, plane, along_zz) if chunk == 0 else (plane, along_zz, along_zz, plane)
         along[stage](*stages[stage], stage * 3 + chunk, pl.ds(*CHUNKS[chunk]))
 
     def arrived(chunk, stage, k=None, rows=None):
@@ -279,7 +262,7 @@
     for k in range(6):
         forward(k)
         if k < 3:
-            z_then(send1, mid1, 0, pl.ds(8 * k, 8))
+            along_zz(send1, mid1, 0, pl.ds(8 * k, 8))
         for j in ((1, 2), (3,), (4,), (5,), (), ())[k]:
             join(j)
 
@@ -306,7 +289,7 @@
     go(1, 3)
     arrived(0, 2)
     for x in range(3):
-        then_z(mid2, recv2, 11 + x if x else 9, pl.ds(8 * x, 8))
+        along_zz(mid2, recv2, 11 + x if x else 9, pl.ds(8 * x, 8))
     arrived(2, 2)
     go(2, 3)
     arrived(1, 3)

time: 99.8 us -> 98.7 us (0.989); the launches traced: 98.4 us -> 98.7 us
  no operation moved by 1% of the time
where the time goes in v9:
time: 98.7 us
  Pallas kernels  97.6 us (99%)
  local copies, waits for them, and re-layouts  1.02 us (1%)
    pallas_call x1, Pallas kernels, shards(): pl.pallas_call(kernel, out_shape=jax.ShapeDtypeStruct((2, PL3, NG, NG), F...  97.6 us

profile of v9, /device:TPU:8, one launch (start us, length us, event | category | flops | bytes accessed | tf_op | source)
XLA Modules:
  0.0 98.7 jit_solution(16167323596599291115)
XLA Ops:
  0.0 97.6 %shard_map.73 = f32[2,3,192,192]{3,2,1,0:T(8,128)S(1)} custom-call(s32[2]{0:T(128)} %occ_index.1, s32[2]{0:T(128)} %band_pick.1, f32[2,3,192,192]{3,2,1,0:T(8,128)} %bands_in.1, f32[4,3,192,192]{3,2,1,0:T(8,128)} %occupied_in.1, bf16[4,2,192,192]{3,2,1,0:T(8,128)(2,1)} %constant.6.clone.rows_in, bf16[2,2,256,256]{3,2,1,0:T(8,128)(2,1)} %constant.7.clone.zmat_in, ...), custom_call_target="tpu_custom_call" | custom-call | tf_op jit(solution)/shard_map/pallas_call | solution.py:320
  97.6 1.0 %copy.9 = f32[2,3,192,192]{3,2,1,0:T(8,128)} copy(f32[2,3,192,192]{3,2,1,0:T(8,128)S(1)} %shard_map.73) | data formatting | bytes 1769472

commit v10 on v9

--- a/solution.py
+++ b/solution.py
@@ -18,7 +18,7 @@
 CHUNKS = ((0, 24), (24, 15), (40, 15))
 BLOCKS = (range(0, 8), range(8, 13), range(13, 18))
 WIDE = 56
-Z_STEPS = (1, 7, 2, 6, 3, 5, 4)
+Z_STEPS = (4, 3, 5, 2, 6, 1, 7)
 
 
 def row_of(n, x):

time: 98.7 us -> 98.5 us (level); the launches traced: 98.7 us -> 97.5 us
  Pallas kernels: 97.6 us -> 96.4 us
    pallas_call x1, Pallas kernels: 97.6 us -> 96.4 us  [shards(): pl.pallas_call(kernel, out_shape=jax.ShapeDtypeStruct((2, PL3, NG, NG), F...]
where the time goes in v10:
time: 98.5 us; the launch traced here: 97.5 us
  Pallas kernels  96.4 us (98%)
  local copies, waits for them, and re-layouts  1.02 us (1%)
    pallas_call x1, Pallas kernels, shards(): pl.pallas_call(kernel, out_shape=jax.ShapeDtypeStruct((2, PL3, NG, NG), F...  96.4 us

profile of v10, /device:TPU:8, one launch (start us, length us, event | category | flops | bytes accessed | tf_op | source)
XLA Modules:
  0.0 97.5 jit_solution(7577923930362469443)
XLA Ops:
  0.0 96.4 %shard_map.73 = f32[2,3,192,192]{3,2,1,0:T(8,128)S(1)} custom-call(s32[2]{0:T(128)} %occ_index.1, s32[2]{0:T(128)} %band_pick.1, f32[2,3,192,192]{3,2,1,0:T(8,128)} %bands_in.1, f32[4,3,192,192]{3,2,1,0:T(8,128)} %occupied_in.1, bf16[4,2,192,192]{3,2,1,0:T(8,128)(2,1)} %constant.6.clone.rows_in, bf16[2,2,256,256]{3,2,1,0:T(8,128)(2,1)} %constant.7.clone.zmat_in, ...), custom_call_target="tpu_custom_call" | custom-call | tf_op jit(solution)/shard_map/pallas_call | solution.py:320
  96.4 1.0 %copy.9 = f32[2,3,192,192]{3,2,1,0:T(8,128)} copy(f32[2,3,192,192]{3,2,1,0:T(8,128)S(1)} %shard_map.73) | data formatting | bytes 1769472
